TPU v7x, 768 devices: a whole 4x8x12 slice. The times are simulated.
768 devices in a mesh: gx: 12 (over z), gy: 64 (over x, y, core).
Axes of the slice: x: 4, y: 8, z: 12, core: 2. Of those that a mesh axis runs over, the one named last changes fastest.
Arguments:
- wavefield: float32 [9, 56, 98304], P(None, None, ('gx', 'gy')), may hold values from -6 to 6
- star_mats: float32 [3, 9, 9, 98304], P(None, None, None, ('gx', 'gy')), may hold values from -1 to 1
- flux_own: float32 [4, 9, 9, 98304], P(None, None, None, ('gx', 'gy')), may hold values from -0.8 to 0.8
- flux_nbr: float32 [4, 9, 9, 98304], P(None, None, None, ('gx', 'gy')), may hold values from -0.8 to 0.8
- stiffness: float32 [3, 56, 56], replicated, may hold values from -0.75 to 0.75
- face_proj: float32 [4, 21, 56], replicated, may hold values from -0.75 to 0.75
- lift_mats: float32 [4, 56, 21], replicated, may hold values from -1.25 to 1.25
- cluster: int32 [98304], P(('gx', 'gy')), may hold values from 0 to 1
- yield_stress: float32 [98304], P(('gx', 'gy')), may hold values from 0.5 to 5
- plastic_mask: int32 [98304], P(('gx', 'gy')), may hold values from 0 to 1
- face_source: int32 [4, 98304], P(None, ('gx', 'gy')), may hold values from 0 to 639, as said below
- send_faces: int32 [3072, 32], P(('gx', 'gy')), may hold values from 0 to 511, as said below
- fault_faces: int32 [768, 64], P(('gx', 'gy')), may hold values from 0 to 511, as said below
- fault_owner: int32 [49152, 1], P(('gx', 'gy')), may hold values from 0 to 63; in each aligned block of 64 rows (0 to 63, 64 to 127, ...) at most 2 rows name the same one
- fault_slip: float32 [98304], P(('gx', 'gy')), may hold values from 0 to 1
- cohesion: float32 [98304], P(('gx', 'gy')), may hold values from 0.1 to 1
- slip_flag: int32 [98304], P(('gx', 'gy')), may hold values from 0 to 1
Outputs:
- wavefield_out: float32 [9, 56, 98304], P(None, None, ('gx', 'gy'))
- slip_out: float32 [98304], P(('gx', 'gy'))
Inputs may be any that keep to these rules, and one draw needn't show every extreme that they name: `face_source`: entries below 512 name the partition's own faces; every received slot is named by exactly one face of its partition. `send_faces`: entries of one row are distinct. `fault_faces`: entries of one partition are distinct. `fault_owner`: among the fault faces of one partition at most 2 name the same owner.
All inputs are finite; a program needn't handle non-finite values.
Results may differ from a plain program's by a relative error of at most 0.0001.
Values sent between devices are 32-bit elements; how exact they have to be, the bound alone decides.
No kernel may reach another device: no remote copies, remote signals or barrier semaphores. Data moves between devices by JAX's collectives and lax.ppermute only.
A program may use at most 64 MiB of HBM per device.

v0:
```python
import jax
import jax.numpy as jnp
from jax import lax
from jax.experimental import pallas as pl
from jax.experimental.pallas import tpu as pltpu
from jax.sharding import PartitionSpec as P

F32 = jnp.float32
BF16 = jnp.bfloat16

VARS = 9
MODES = 56
FACE_PTS = 21
ORDER = 6
FACES = 4
E = 128
SLOTS = 32
PTS = 24
ROWS = 224
MSG = ROWS // 4
WIDE = VARS * E


def halves(x):
    top = x.astype(BF16)
    return top, (x - top.astype(F32)).astype(BF16)


def dot(a, b):
    return jnp.dot(a, b, preferred_element_type=F32)


def iota(shape, dim):
    return lax.broadcasted_iota(jnp.int32, shape, dim)


def one_hot(mask):
    return jnp.where(mask, 1.0, 0.0).astype(BF16)


def lanes(w):
    return slice(E * w, E * (w + 1))


def widen(x):
    top = x.astype(BF16).astype(F32)
    rest = x - top
    pair = [part + pltpu.roll(part, 64, 1) for part in (top, rest)]
    return jnp.concatenate(pair, axis=1).astype(BF16)


def stack_stiffness(stiff_ref, tall_ref):
    tall_ref[...] = jnp.zeros_like(tall_ref)
    for d in range(3):
        tall_ref[MODES * d : MODES * (d + 1), 0:MODES] = stiff_ref[d]
    return widen(tall_ref[...])


def stack_stiffness_t(stiff_ref, tall_ref, square_ref):
    square_ref[...] = jnp.zeros_like(square_ref)
    for d in range(3):
        square_ref[0:MODES, 0:MODES] = stiff_ref[d]
        tall_ref[MODES * d : MODES * (d + 1), :] = jnp.transpose(square_ref[...])[0:MODES]
    return widen(tall_ref[...])


def spread_faces(face_ref, square_ref):
    square_ref[...] = jnp.zeros_like(square_ref)
    for f in range(FACES):
        for j in range(FACE_PTS):
            square_ref[PTS * f + j : PTS * f + j + 1, 0:MODES] = face_ref[j, f : f + 1, :]


def load_rhs(read, rhs_ref):
    pad = jnp.zeros((64 - MODES, E), F32)
    for w in range(VARS):
        x = read(w)
        top = x.astype(BF16).astype(F32)
        high = jnp.concatenate([top, pad], axis=0).astype(BF16)
        low = jnp.concatenate([x - top, pad], axis=0).astype(BF16)
        rhs_ref[0:64, lanes(w)] = high
        rhs_ref[64:128, lanes(w)] = low
        rhs_ref[128:192, lanes(w)] = high
        rhs_ref[192:256, lanes(w)] = low


def product(a, rhs_ref, out_ref):
    for start in range(0, WIDE, 256):
        cols = slice(start, min(start + 256, WIDE))
        out_ref[:, cols] = dot(a, rhs_ref[:, cols])


def star_mix(star_ref, tall_ref, emit):
    def body(group, carry):
        sums = [jnp.zeros((MODES, E), F32) for _ in range(3)]
        for w in range(VARS):
            for d in range(3):
                x = tall_ref[MODES * d : MODES * (d + 1), lanes(w)]
                for i in range(3):
                    sums[i] = sums[i] + star_ref[3 * group + i, w, d : d + 1, :] * x
        for i in range(3):
            emit(3 * group + i, sums[i])
        return carry

    lax.fori_loop(0, 3, body, 0)


def predict(start_ref, star_ref, left, deriv_ref, rhs_ref, tall_ref, early_ref, late_ref):
    early_ref[...] = start_ref[...]
    if late_ref is not None:
        late_ref[...] = start_ref[...]
    factor = 1.0
    for power in range(2, ORDER + 1):
        factor = factor * power
        source = start_ref if power == 2 else deriv_ref
        load_rhs(lambda w: source[w], rhs_ref)
        product(left, rhs_ref, tall_ref)
        to_early = 1.0 / factor
        to_late = (2.0**power - 1.0) / factor

        def emit(v, change):
            if power < ORDER:
                deriv_ref[v] = -change
            early_ref[v] = early_ref[v] - change * to_early
            if late_ref is not None:
                late_ref[v] = late_ref[v] - change * to_late

        star_mix(star_ref, tall_ref, emit)


def direction_rows(send_ref):
    rows = [send_ref[d : d + 1, :] for d in range(4)]
    order = []
    for axis, base in (("gx", 0), ("gy", 2)):
        odd = lax.axis_index(axis) % 2 == 1
        order.append(jnp.where(odd, rows[base], rows[base + 1]))
        order.append(jnp.where(odd, rows[base + 1], rows[base]))
    return order


def make_traces(left, integral_ref, rhs_ref, own_ref, table_ref, high_ref, low_ref):
    load_rhs(lambda w: integral_ref[w], rhs_ref)
    product(left, rhs_ref, own_ref)
    for w in range(VARS):
        for f in range(FACES):
            table_ref[PTS * w : PTS * (w + 1), lanes(f)] = own_ref[PTS * f : PTS * (f + 1), lanes(w)]
    table_ref[PTS * VARS : ROWS, :] = jnp.zeros((ROWS - PTS * VARS, FACES * E), F32)
    high, low = halves(table_ref[...])
    high_ref[...] = high
    low_ref[...] = low


def make_messages(send_ref, high_ref, low_ref, out_refs):
    listed = jnp.concatenate(direction_rows(send_ref), axis=1)
    pick = one_hot(iota((FACES * E, 4 * SLOTS), 0) == listed)
    picked = dot(high_ref[...], pick) + dot(low_ref[...], pick)
    turned = [picked] + [pltpu.roll(picked, SLOTS * k, 1) for k in range(1, 4)]
    part = iota((MSG, E), 1) // SLOTS
    for b in range(4):
        packed = turned[(0 - b) % 4][0:MSG]
        for q in range(1, 4):
            packed = jnp.where(part == q, turned[(q - b) % 4][MSG * q : MSG * (q + 1)], packed)
        out_refs[b][...] = packed


def unpack_messages(in_refs):
    part = iota((MSG, E), 1) // SLOTS
    blocks = []
    for q in range(4):
        block = None
        for b in range(4):
            shift = (SLOTS * (b - q)) % E
            x = in_refs[b][...]
            x = pltpu.roll(x, shift, 1) if shift else x
            block = x if block is None else jnp.where(part == b, x, block)
        blocks.append(block)
    return jnp.concatenate(blocks, axis=0)


def received_slots(source_ref):
    slot = source_ref[...] - FACES * E
    swap_x = SLOTS * (1 - lax.axis_index("gx") % 2)
    swap_y = SLOTS * (1 - lax.axis_index("gy") % 2)
    swap = jnp.where(slot < 2 * SLOTS, swap_x, swap_y)
    return jnp.where(slot < 0, slot, slot ^ swap)


def finish_gather(source_ref, message_refs, near_ref, nbr_ref):
    slots = received_slots(source_ref)
    high, low = halves(unpack_messages(message_refs))
    for f in range(FACES):
        pick = one_hot(iota((4 * SLOTS, E), 0) == slots[f : f + 1])
        far = dot(high, pick) + dot(low, pick)
        nbr_ref[:, lanes(f)] = near_ref[:, lanes(f)] + far


def face_state(own_ref, nbr_ref, faces_row, state_ref):
    for c, (t, s) in enumerate(((0, 6), (3, 7), (5, 8))):
        for f in range(FACES):
            own_t = own_ref[PTS * f : PTS * (f + 1), lanes(t)]
            own_v = own_ref[PTS * f : PTS * (f + 1), lanes(s)]
            nbr_t = nbr_ref[PTS * t : PTS * (t + 1), lanes(f)]
            nbr_v = nbr_ref[PTS * s : PTS * (s + 1), lanes(f)]
            state_ref[PTS * c : PTS * (c + 1), lanes(f)] = 0.5 * (own_t + nbr_t) + 0.5 * (nbr_v - own_v)
    high, low = halves(state_ref[...])
    pick = one_hot(iota((FACES * E, faces_row.shape[1]), 0) == faces_row)
    return dot(high, pick) + dot(low, pick)


def column_of(row):
    count = row.shape[1]
    diagonal = iota((count, count), 0) == iota((count, count), 1)
    return jnp.sum(jnp.where(diagonal, row.astype(F32), 0.0), axis=1, keepdims=True)


def owner_masks(owner_row, gy_size):
    count = owner_row.shape[1]
    owner_col = column_of(owner_row)
    same = owner_col == owner_row.astype(F32)
    earlier = iota((count, count), 0) < iota((count, count), 1)
    rank = jnp.sum(jnp.where(same & earlier, 1.0, 0.0), axis=0, keepdims=True)
    named = iota((gy_size, count), 0) == owner_row
    return named, rank


def slot_values(params_ref, named, rank):
    out = []
    for c in range(3):
        both = []
        for r in range(2):
            col = params_ref[:, 3 * r + c : 3 * r + c + 1]
            both.append(jnp.sum(jnp.where(named, col, 0.0), axis=0, keepdims=True))
        out.append(jnp.where(rank > 0.5, both[1], both[0]))
    return out


def friction(state, slip, cohesion, flag):
    coeff = 0.6 - 0.3 * jnp.minimum(slip / 0.5, 1.0)
    normal, first, second = (state[PTS * c : PTS * (c + 1)] for c in range(3))
    strength = cohesion + coeff * jnp.maximum(-normal, 0.0)
    magnitude = jnp.sqrt(first * first + second * second)
    ratio = jnp.where(flag > 0.5, strength / jnp.maximum(magnitude, strength), 1.0)
    change = jnp.concatenate([first * (ratio - 1.0), second * (ratio - 1.0)], axis=0)
    slip_new = slip + jnp.sum(magnitude * (1.0 - ratio), axis=0, keepdims=True) / FACE_PTS
    return change, slip_new


def spread_change(change, faces_row):
    count = faces_row.shape[1]
    faces_col = column_of(faces_row)
    place = one_hot(iota((count, FACES * E), 1).astype(F32) == faces_col)
    high, low = halves(change)
    return dot(high, place) + dot(low, place)


def mix_faces(mats_ref, trace, start, flux_ref):
    def body(v, carry):
        cols = pl.ds(pl.multiple_of(v * E, E), E)
        for f in range(FACES):
            rows = slice(PTS * f, PTS * (f + 1))
            total = None if start is None else start[rows, cols]
            for w in range(VARS):
                term = mats_ref[v, w, f : f + 1, :] * trace(f, w)
                total = term if total is None else total + term
            flux_ref[rows, cols] = total
        return carry

    lax.fori_loop(0, VARS, body, 0)


def lift(lift_ref, flux_ref, out_ref):
    top = lift_ref[0][:, 0 : FACES * PTS]
    rest = lift_ref[1][:, 0 : FACES * PTS]
    for start in range(0, WIDE, 256):
        cols = slice(start, min(start + 256, WIDE))
        high, low = halves(flux_ref[:, cols])
        out_ref[:, cols] = dot(top, high) + (dot(top, low) + dot(rest, high))


def add_change(flux_ref, delta):
    for c, v in ((0, 3), (1, 5)):
        for f in range(FACES):
            rows = slice(PTS * f, PTS * (f + 1))
            flux_ref[rows, lanes(v)] = flux_ref[rows, lanes(v)] + delta[PTS * c : PTS * (c + 1), lanes(f)]


def plastic(read, mask_row, yield_row):
    q = [read(v) for v in range(6)]
    mean = (q[0] + q[1] + q[2]) / 3.0
    dev = [x - mean for x in q[0:3]]
    dev_sq = dev[0] * dev[0] + dev[1] * dev[1] + dev[2] * dev[2]
    shear_sq = q[3] * q[3] + q[4] * q[4] + q[5] * q[5]
    second = jnp.sum(dev_sq + 2.0 * shear_sq, axis=0, keepdims=True) / (2.0 * MODES)
    equiv = jnp.sqrt(second + 1e-06)
    factor = 1.0 - mask_row.astype(F32) * 0.5 * jnp.maximum(1.0 - yield_row / equiv, 0.0)
    return [mean + factor * x for x in dev] + [factor * x for x in q[3:6]]


def params_kernel(slip_ref, cohesion_ref, flag_ref, out_ref):
    gy_size = out_ref.shape[0]
    shape = (gy_size, slip_ref.shape[1])
    cols = []
    for r in range(2):
        mine = iota(shape, 1) == 2 * iota(shape, 0) + r
        for row in (slip_ref[...], cohesion_ref[...], flag_ref[...].astype(F32)):
            cols.append(jnp.sum(jnp.where(mine, row, 0.0), axis=1, keepdims=True))
    column = iota(out_ref.shape, 1)
    out = jnp.zeros(out_ref.shape, F32)
    for i, col in enumerate(cols):
        out = jnp.where(column == i, col, out)
    out_ref[...] = out


def slip_kernel(in_ref, out_ref):
    shape = (in_ref.shape[0], out_ref.shape[1])
    out = jnp.zeros((1, shape[1]), F32)
    for r in range(2):
        mine = iota(shape, 1) == 2 * iota(shape, 0) + r
        out = out + jnp.sum(jnp.where(mine, in_ref[:, r : r + 1], 0.0), axis=0, keepdims=True)
    out_ref[...] = out


def first_kernel(
    wave_ref, star_ref, stiff_ref, proj_ref, send_ref,
    early_ref, late_ref, own_ref, high_ref, low_ref, m0, m1, m2, m3, ap_ref, at_ref,
    deriv_ref, rhs_ref, tall_ref, lhs_ref, square_ref, table_ref,
):
    ap_ref[...] = stack_stiffness(stiff_ref, lhs_ref)
    spread_faces(proj_ref, square_ref)
    at_ref[...] = widen(square_ref[0 : FACES * PTS])
    predict(wave_ref, star_ref, ap_ref[...], deriv_ref, rhs_ref, tall_ref, early_ref, late_ref)
    make_traces(at_ref[...], early_ref, rhs_ref, own_ref, table_ref, high_ref, low_ref)
    make_messages(send_ref, high_ref, low_ref, (m0, m1, m2, m3))


def near_work(integral_ref, star_ref, own_mats_ref, own_ref, high_ref, low_ref, source_ref, left,
              vol_ref, flux_ref, near_ref, rhs_ref, tall_ref):
    load_rhs(lambda w: integral_ref[w], rhs_ref)
    product(left, rhs_ref, tall_ref)

    def emit(v, total):
        vol_ref[v] = total

    star_mix(star_ref, tall_ref, emit)
    mix_faces(own_mats_ref, lambda f, w: own_ref[PTS * f : PTS * (f + 1), lanes(w)], None, flux_ref)
    for f in range(FACES):
        pick = one_hot(iota((FACES * E, E), 0) == source_ref[f : f + 1, :])
        near_ref[:, lanes(f)] = dot(high_ref[...], pick) + dot(low_ref[...], pick)


def near_first_kernel(
    integral_ref, star_ref, own_mats_ref, own_ref, high_ref, low_ref, source_ref, stiff_ref, lift_ref,
    vol_ref, flux_ref, near_ref, av_ref, al_ref,
    rhs_ref, tall_ref, lhs_ref, square_ref,
):
    av_ref[...] = stack_stiffness_t(stiff_ref, lhs_ref, square_ref)
    spread_faces(lift_ref, square_ref)
    high, low = halves(jnp.transpose(square_ref[...])[0:MODES])
    al_ref[0] = high
    al_ref[1] = low
    near_work(integral_ref, star_ref, own_mats_ref, own_ref, high_ref, low_ref, source_ref, av_ref[...],
              vol_ref, flux_ref, near_ref, rhs_ref, tall_ref)


def near_second_kernel(
    integral_ref, star_ref, own_mats_ref, own_ref, high_ref, low_ref, source_ref, av_ref,
    vol_ref, flux_ref, near_ref,
    rhs_ref, tall_ref,
):
    near_work(integral_ref, star_ref, own_mats_ref, own_ref, high_ref, low_ref, source_ref, av_ref[...],
              vol_ref, flux_ref, near_ref, rhs_ref, tall_ref)


def middle_kernel(
    wave_ref, late_ref, vol_ref, part_ref, near_ref, own_ref, m0, m1, m2, m3, nbr_mats_ref, source_ref,
    faces_ref, owner_ref, params_ref, star_ref, ap_ref, at_ref, al_ref, send_ref, cluster_ref, yield_ref, mask_ref,
    integral_ref, base_ref, own2_ref, high_ref, low_ref, n0, n1, n2, n3, par_ref,
    nbr_ref, state_ref, flux_ref, lifted_ref, mid_ref, deriv_ref, rhs_ref, tall_ref, table_ref,
):
    finish_gather(source_ref, (m0, m1, m2, m3), near_ref, nbr_ref)
    faces_row = faces_ref[...]
    state = face_state(own_ref, nbr_ref, faces_row, state_ref)
    named, rank = owner_masks(owner_ref[...], params_ref.shape[0])
    slip, cohesion, flag = slot_values(params_ref, named, rank)
    change, slip_new = friction(state, slip, cohesion, flag)
    par_ref[0:1, :] = slip_new
    par_ref[1:2, :] = cohesion
    par_ref[2:3, :] = flag
    delta = spread_change(change, faces_row)
    mix_faces(
        nbr_mats_ref, lambda f, w: nbr_ref[PTS * w : PTS * (w + 1), lanes(f)], part_ref, flux_ref
    )
    add_change(flux_ref, delta)
    lift(al_ref, flux_ref, lifted_ref)
    coarse = cluster_ref[...] == 1
    for v in range(VARS):
        increment = vol_ref[v] - lifted_ref[:, lanes(v)]
        mid_ref[v] = wave_ref[v] + increment
        base_ref[v] = jnp.where(coarse, increment, 0.0)
    stressed = plastic(lambda v: mid_ref[v], mask_ref[...], yield_ref[...])
    for v in range(VARS):
        fine = stressed[v] if v < 6 else mid_ref[v]
        midway = jnp.where(coarse, wave_ref[v], fine)
        mid_ref[v] = midway
        base_ref[v] = midway + base_ref[v]
    predict(mid_ref, star_ref, ap_ref[...], deriv_ref, rhs_ref, tall_ref, integral_ref, None)
    for v in range(VARS):
        integral_ref[v] = jnp.where(coarse, late_ref[v], integral_ref[v])
    make_traces(at_ref[...], integral_ref, rhs_ref, own2_ref, table_ref, high_ref, low_ref)
    make_messages(send_ref, high_ref, low_ref, (n0, n1, n2, n3))


def fault_kernel(
    near_ref, own_ref, m0, m1, m2, m3, source_ref, faces_ref, owner_ref, params_ref, par_ref,
    nbr_ref, delta_ref, back_ref,
    state_ref,
):
    finish_gather(source_ref, (m0, m1, m2, m3), near_ref, nbr_ref)
    faces_row = faces_ref[...]
    state = face_state(own_ref, nbr_ref, faces_row, state_ref)
    change, slip_new = friction(state, par_ref[0:1, :], par_ref[1:2, :], par_ref[2:3, :])
    delta_ref[...] = spread_change(change, faces_row)
    named, rank = owner_masks(owner_ref[...], params_ref.shape[0])
    column = iota(back_ref.shape, 1)
    out = jnp.zeros(back_ref.shape, F32)
    for r in range(2):
        here = named & ((rank > 0.5) == (r == 1))
        total = jnp.sum(jnp.where(here, slip_new, 0.0), axis=1, keepdims=True)
        used = jnp.sum(jnp.where(here, 1.0, 0.0), axis=1, keepdims=True)
        value = jnp.where(used > 0.5, total, params_ref[:, 3 * r : 3 * r + 1])
        out = jnp.where(column == r, value, out)
    back_ref[...] = out


def last_kernel(
    base_ref, vol_ref, part_ref, nbr_ref, delta_ref, nbr_mats_ref, al_ref, yield_ref, mask_ref,
    out_ref,
    flux_ref, lifted_ref,
):
    mix_faces(
        nbr_mats_ref, lambda f, w: nbr_ref[PTS * w : PTS * (w + 1), lanes(f)], part_ref, flux_ref
    )
    add_change(flux_ref, delta_ref[...])
    lift(al_ref, flux_ref, lifted_ref)
    for v in range(VARS):
        out_ref[v] = base_ref[v] + (vol_ref[v] - lifted_ref[:, lanes(v)])
    stressed = plastic(lambda v: out_ref[v], mask_ref[...], yield_ref[...])
    for v in range(6):
        out_ref[v] = stressed[v]


def shape(dims, dtype=F32):
    return jax.ShapeDtypeStruct(dims, dtype)


def call(kernel, outs, scratch=()):
    return pl.pallas_call(
        kernel,
        out_shape=outs,
        scratch_shapes=[pltpu.VMEM(dims, dtype) for dims, dtype in scratch],
    )


FIELD = (VARS, MODES, E)
TRACE = (FACES * PTS, WIDE)
TABLE = (ROWS, FACES * E)
LEFT = (3 * MODES, 256)
TALL = (3 * MODES, WIDE)
RHS = (256, WIDE)


def pair_up(x, axis, odd):
    count = lax.axis_size(axis)
    if odd:
        pairs = [(i, (i + 1) % count if i % 2 else (i - 1) % count) for i in range(count)]
    else:
        pairs = [(i, i ^ 1) for i in range(count)]
    return lax.ppermute(x, axis, pairs)


def exchange(messages):
    return [pair_up(x, axis, odd) for x, (axis, odd) in zip(messages, (("gx", 0), ("gx", 1), ("gy", 0), ("gy", 1)))]


def local(
    wavefield,
    star_mats,
    flux_own,
    flux_nbr,
    stiffness,
    face_proj,
    lift_mats,
    cluster,
    yield_stress,
    plastic_mask,
    face_source,
    send_faces,
    fault_faces,
    fault_owner,
    fault_slip,
    cohesion,
    slip_flag,
):
    gy_size = lax.axis_size("gy")
    faults = fault_faces.shape[1]
    slot_count = fault_slip.shape[0]
    star = jnp.transpose(star_mats, (1, 2, 0, 3))
    own_mats = jnp.transpose(flux_own, (1, 2, 0, 3))
    nbr_mats = jnp.transpose(flux_nbr, (1, 2, 0, 3))
    proj = jnp.transpose(face_proj, (1, 0, 2))
    lifts = jnp.transpose(lift_mats, (2, 0, 1))
    owner = jnp.transpose(fault_owner)
    cluster, yield_stress, plastic_mask = (x.reshape(1, E) for x in (cluster, yield_stress, plastic_mask))
    slots = [x.reshape(1, slot_count) for x in (fault_slip, cohesion, slip_flag)]

    params = call(params_kernel, shape((gy_size, 8)))(*slots)
    params = lax.all_to_all(params, "gy", 0, 0, tiled=True)

    messages = [shape((MSG, E))] * 4
    work = [(FIELD, F32), (RHS, BF16), (TALL, F32)]
    early, late, own, high, low, m0, m1, m2, m3, ap, at = call(
        first_kernel,
        [shape(FIELD), shape(FIELD), shape(TRACE), shape(TABLE, BF16), shape(TABLE, BF16), *messages,
         shape(LEFT, BF16), shape((FACES * PTS, 256), BF16)],
        work + [((3 * MODES, E), F32), ((E, E), F32), (TABLE, F32)],
    )(wavefield, star, stiffness, proj, send_faces)
    got = exchange((m0, m1, m2, m3))
    vol, part, near, av, al = call(
        near_first_kernel,
        [shape(FIELD), shape(TRACE), shape(TABLE), shape(LEFT, BF16), shape((2, MODES, E), BF16)],
        work[1:] + [((3 * MODES, E), F32), ((E, E), F32)],
    )(early, star, own_mats, own, high, low, face_source, stiffness, lifts)
    integral, base, own, high, low, m0, m1, m2, m3, par = call(
        middle_kernel,
        [shape(FIELD), shape(FIELD), shape(TRACE), shape(TABLE, BF16), shape(TABLE, BF16), *messages,
         shape((8, faults))],
        [(TABLE, F32), ((3 * PTS + 8, FACES * E), F32), (TRACE, F32), ((MODES, WIDE), F32), (FIELD, F32)]
        + work + [(TABLE, F32)],
    )(wavefield, late, vol, part, near, own, *got, nbr_mats, face_source, fault_faces, owner, params, star,
      ap, at, al, send_faces, cluster, yield_stress, plastic_mask)
    got = exchange((m0, m1, m2, m3))
    vol, part, near = call(
        near_second_kernel, [shape(FIELD), shape(TRACE), shape(TABLE)], work[1:]
    )(integral, star, own_mats, own, high, low, face_source, av)
    nbr, delta, back = call(
        fault_kernel,
        [shape(TABLE), shape((2 * PTS, FACES * E)), shape((gy_size, 8))],
        [((3 * PTS + 8, FACES * E), F32)],
    )(near, own, *got, face_source, fault_faces, owner, params, par)
    back = lax.all_to_all(back, "gy", 0, 0, tiled=True)
    out = call(last_kernel, shape(FIELD), [(TRACE, F32), ((MODES, WIDE), F32)])(
        base, vol, part, nbr, delta, nbr_mats, al, yield_stress, plastic_mask
    )
    slip_out = call(slip_kernel, shape((1, slot_count)))(back)
    return (out, slip_out.reshape(slot_count))


def solution(mesh):
    flat = ("gx", "gy")
    last2, last3, last1 = P(None, None, flat), P(None, None, None, flat), P(flat)
    return jax.shard_map(
        local,
        mesh=mesh,
        in_specs=(
            last2, last3, last3, last3, P(), P(), P(), last1, last1, last1,
            P(None, flat), P(flat, None), P(flat, None), P(flat, None), last1, last1, last1,
        ),
        out_specs=(last2, last1),
        check_vma=False,
    )
```

profile of v0, /device:TPU:1, one launch (start us, length us, event | category | flops | bytes accessed | tf_op | source)
XLA Modules:
  0.0 97.3 jit_solution(15259518370374165488)
XLA Ops:
  0.6 7.3 %shard_map.176 = (f32[9,56,128]{2,1,0:T(8,128)}, f32[9,56,128]{2,1,0:T(8,128)}, f32[96,1152]{1,0:T(8,128)}, bf16[224,512]{1,0:T(8,128)(2,1)}, bf16[224,512]{1,0:...) custom-call(f32[9,56,128]{2,1,0:T(8,128)} %wave_ref.3, ...), custom_call_target="tpu_custom_call" | custom-call | tf_op jit(solution)/shard_map/pallas_call | solution.py:521
  8.0 4.8 %collective-permute-start = (f32[56,128]{1,0:T(8,128)}, f32[56,128]{1,0:T(8,128)S(1)}, u32[]{:S(2)}, u32[]{:S(2)}) collective-permute-start(f32[56,128]{1,0:T(8,128)} %get-tuple-element.42), channel_id=1, source_target_pairs={{0,64},{64,0},{128,192},{192,128},{256,320},{320,256},{384,448},{4... | collective-permute-start | bytes 86024 | tf_op jit(solution)/shard_map/ppermute | solution.py:478
  12.8 12.5 %collective-permute-start.1 = (f32[56,128]{1,0:T(8,128)}, f32[56,128]{1,0:T(8,128)S(1)}, u32[]{:S(2)}, u32[]{:S(2)}) collective-permute-start(f32[56,128]{1,0:T(8,128)} %get-tuple-element.43), channel_id=1, source_target_pairs={{0,704},{64,128},{128,64},{192,256},{256,192},{320,384},{384,320},... | collective-permute-start | bytes 86024 | tf_op jit(solution)/shard_map/ppermute | solution.py:478
  25.3 3.1 %collective-permute-start.2 = (f32[56,128]{1,0:T(8,128)}, f32[56,128]{1,0:T(8,128)S(1)}, u32[]{:S(2)}, u32[]{:S(2)}) collective-permute-start(f32[56,128]{1,0:T(8,128)} %get-tuple-element.44), channel_id=1, source_target_pairs={{0,1},{1,0},{2,3},{3,2},{4,5},{5,4},{6,7},{7,6},{8,9},{9,8},{10,11... | collective-permute-start | bytes 86024 | tf_op jit(solution)/shard_map/ppermute | solution.py:478
  28.4 3.1 %collective-permute-start.3 = (f32[56,128]{1,0:T(8,128)}, f32[56,128]{1,0:T(8,128)S(1)}, u32[]{:S(2)}, u32[]{:S(2)}) collective-permute-start(f32[56,128]{1,0:T(8,128)} %get-tuple-element.45), channel_id=1, source_target_pairs={{0,63},{1,2},{2,1},{3,4},{4,3},{5,6},{6,5},{7,8},{8,7},{9,10},{10,... | collective-permute-start | bytes 86024 | tf_op jit(solution)/shard_map/ppermute | solution.py:478
  31.5 1.4 %shard_map.178 = f32[64,8]{1,0:T(8,128)} custom-call(f32[1,128]{1,0:T(1,128)} %bitcast.42, f32[1,128]{1,0:T(1,128)} %bitcast.43, s32[1,128]{1,0:T(1,128)} %bitcast.44), custom_call_target="tpu_custom_call" | custom-call | tf_op jit(solution)/shard_map/pallas_call | solution.py:516
  32.9 9.6 %all-to-all-start = ((f32[64,1,8]{2,1,0:T(1,128)}), f32[64,1,8]{2,1,0:T(1,128)S(1)}, u32[]{:S(2)}, u32[]{:S(2)}) async-start(f32[64,1,8]{2,1,0:T(1,128)} %bitcast.32), calls=%async_computation | async-start | bytes 65536 | tf_op jit(solution)/shard_map/all_to_all | solution.py:517
  42.6 4.3 %shard_map.177 = (f32[9,56,128]{2,1,0:T(8,128)}, f32[96,1152]{1,0:T(8,128)}, f32[224,512]{1,0:T(8,128)}, bf16[168,256]{1,0:T(8,128)(2,1)}, bf16[2,56,128]{2,1,0:T(8,128)(2,1)}) custom-call(f32[9,56,128]{2,1,0:T(8,128)} %get-tuple-element.35.integral_ref, f32[9,9,3,128]{3,2,1,0:T(4,128)} %bitcast.22, f32[9,9,4,128]{3,2,1,0:T(4,128)} %bitcast.25, ...), custom_call_target="tpu_custom_call" | custom-call | tf_op jit(solution)/shard_map/pallas_call | solution.py:528
  46.8 5.0 %all-to-all-done = f32[64,1,8]{2,1,0:T(1,128)S(1)} async-done(((f32[64,1,8]{2,1,0:T(1,128)}), f32[64,1,8]{2,1,0:T(1,128)S(1)}, u32[]{:S(2)}, u32[]{:S(2)}) %all-to-all-start) | async-done | bytes 2080 | tf_op jit(solution)/shard_map/all_to_all | solution.py:517
  51.9 0.0 copy-start
  51.9 0.0 collective-permute-done.m0
  51.9 0.0 copy-start.6
  51.9 0.0 collective-permute-done.1.m1
  51.9 0.0 copy-start.7
  51.9 0.0 collective-permute-done.2.m2
  51.9 0.0 copy-start.8
  51.9 0.0 collective-permute-done.3.m3
  51.9 0.0 copy-start.9
  51.9 0.5 copy-done
  52.5 0.0 copy-done.6
  52.5 0.0 copy-done.7
  52.5 0.0 copy-done.8
  52.5 0.0 copy-done.9
  52.5 9.4 %shard_map.179 = (f32[9,56,128]{2,1,0:T(8,128)}, f32[9,56,128]{2,1,0:T(8,128)}, f32[96,1152]{1,0:T(8,128)}, bf16[224,512]{1,0:T(8,128)(2,1)}, bf16[224,512]{1,0:...) custom-call(f32[9,56,128]{2,1,0:T(8,128)} %wave_ref.3, ...), custom_call_target="tpu_custom_call" | custom-call | tf_op jit(solution)/shard_map/pallas_call | solution.py:533
  61.9 1.9 %collective-permute-start.4 = (f32[56,128]{1,0:T(8,128)}, f32[56,128]{1,0:T(8,128)S(1)}, u32[]{:S(2)}, u32[]{:S(2)}) collective-permute-start(f32[56,128]{1,0:T(8,128)} %get-tuple-element.58), channel_id=1, source_target_pairs={{0,64},{64,0},{128,192},{192,128},{256,320},{320,256},{384,448},{4... | collective-permute-start | bytes 86024 | tf_op jit(solution)/shard_map/ppermute | solution.py:478
  63.8 2.8 %collective-permute-start.5 = (f32[56,128]{1,0:T(8,128)}, f32[56,128]{1,0:T(8,128)S(1)}, u32[]{:S(2)}, u32[]{:S(2)}) collective-permute-start(f32[56,128]{1,0:T(8,128)} %get-tuple-element.59), channel_id=1, source_target_pairs={{0,704},{64,128},{128,64},{192,256},{256,192},{320,384},{384,320},... | collective-permute-start | bytes 86024 | tf_op jit(solution)/shard_map/ppermute | solution.py:478
  66.7 3.1 %collective-permute-start.6 = (f32[56,128]{1,0:T(8,128)}, f32[56,128]{1,0:T(8,128)S(1)}, u32[]{:S(2)}, u32[]{:S(2)}) collective-permute-start(f32[56,128]{1,0:T(8,128)} %get-tuple-element.60), channel_id=1, source_target_pairs={{0,1},{1,0},{2,3},{3,2},{4,5},{5,4},{6,7},{7,6},{8,9},{9,8},{10,11... | collective-permute-start | bytes 86024 | tf_op jit(solution)/shard_map/ppermute | solution.py:478
  69.8 2.2 %collective-permute-start.7 = (f32[56,128]{1,0:T(8,128)}, f32[56,128]{1,0:T(8,128)S(1)}, u32[]{:S(2)}, u32[]{:S(2)}) collective-permute-start(f32[56,128]{1,0:T(8,128)} %get-tuple-element.61), channel_id=1, source_target_pairs={{0,63},{1,2},{2,1},{3,4},{4,3},{5,6},{6,5},{7,8},{8,7},{9,10},{10,... | collective-permute-start | bytes 86024 | tf_op jit(solution)/shard_map/ppermute | solution.py:478
  72.0 4.1 %shard_map.180 = (f32[9,56,128]{2,1,0:T(8,128)}, f32[96,1152]{1,0:T(8,128)}, f32[224,512]{1,0:T(8,128)}) custom-call(f32[9,56,128]{2,1,0:T(8,128)} %get-tuple-element.50.integral_ref, f32[9,9,3,128]{3,2,1,0:T(4,128)} %bitcast.24, f32[9,9,4,128]{3,2,1,0:T(4,128)} %bitcast.26, f32[96,1152]{1,0:T(8,128)} %get-tuple-element.51.own_ref, ...), custom_call_target="tpu_custom_call" | custom-call | tf_op jit(solution)/shard_map/pallas_call | solution.py:542
  76.0 0.0 collective-permute-done.4.m0
  76.0 0.0 copy-start.2
  76.0 0.0 collective-permute-done.5.m1
  76.0 0.0 copy-start.3
  76.1 0.0 collective-permute-done.6.m2
  76.1 0.0 copy-start.4
  76.1 0.0 collective-permute-done.7.m3
  76.1 0.0 copy-start.5
  76.1 0.5 copy-done.2
  76.6 0.0 copy-done.3
  76.7 0.0 copy-done.4
  76.7 0.0 copy-done.5
  76.7 2.6 %shard_map.181 = (f32[224,512]{1,0:T(8,128)}, f32[48,512]{1,0:T(8,128)}, f32[64,8]{1,0:T(8,128)}) custom-call(f32[224,512]{1,0:T(8,128)} %get-tuple-element.57.near_ref, f32[96,1152]{1,0:T(8,128)} %get-tuple-element.51.own_ref, f32[56,128]{1,0:T(8,128)} %copy-done.2, f32[56,128]{1,0:T(8,128)} %copy-done.3, f32[56,128]{1,0:T(8,128)} %copy-done.4, ...), custom_call_target="tpu_custom_call" | custom-call | tf_op jit(solution)/shard_map/pallas_call | solution.py:545
  79.3 6.7 %all-to-all-start.1 = ((f32[64,1,8]{2,1,0:T(1,128)}), f32[64,1,8]{2,1,0:T(1,128)S(1)}, u32[]{:S(2)}, u32[]{:S(2)}) async-start(f32[64,1,8]{2,1,0:T(1,128)} %bitcast.35), calls=%async_computation.1 | async-start | bytes 65536 | tf_op jit(solution)/shard_map/all_to_all | solution.py:550
  86.0 2.9 %shard_map.182 = f32[9,56,128]{2,1,0:T(8,128)} custom-call(f32[9,56,128]{2,1,0:T(8,128)} %get-tuple-element.49.base_ref, f32[9,56,128]{2,1,0:T(8,128)} %get-tuple-element.55.vol_ref, f32[96,1152]{1,0:T(8,128)} %get-tuple-element.56.part_ref, f32[224,512]{1,0:T(8,128)} %get-tuple-element.63.nbr_ref, f32[48,512]{1,0:T(8,128)} %get-tuple-element.64.delta_ref, ...), custom_call_target="tpu_custom_call" | custom-call | tf_op jit(solution)/shard_map/pallas_call | solution.py:551
  88.9 6.4 %all-to-all-done.1 = f32[64,1,8]{2,1,0:T(1,128)S(1)} async-done(((f32[64,1,8]{2,1,0:T(1,128)}), f32[64,1,8]{2,1,0:T(1,128)S(1)}, u32[]{:S(2)}, u32[]{:S(2)}) %all-to-all-start.1) | async-done | bytes 2080 | tf_op jit(solution)/shard_map/all_to_all | solution.py:550
  95.3 0.0 copy-start.1
  95.3 0.6 copy-done.1
  95.9 1.4 %shard_map.183 = f32[1,128]{1,0:T(1,128)} custom-call(f32[64,8]{1,0:T(8,128)} %bitcast.31), custom_call_target="tpu_custom_call" | custom-call | tf_op jit(solution)/shard_map/pallas_call | solution.py:554
Async XLA Ops:
  8.0 43.9 %collective-permute-start = (f32[56,128]{1,0:T(8,128)}, f32[56,128]{1,0:T(8,128)S(1)}, u32[]{:S(2)}, u32[]{:S(2)}) collective-permute-start(f32[56,128]{1,0:T(8,128)} %get-tuple-element.42), channel_id=1, source_target_pairs={{0,64},{64,0},{128,192},{192,128},{256,320},{320,256},{384,448},{4... | collective-permute-start | bytes 86024 | tf_op jit(solution)/shard_map/ppermute | solution.py:478
  12.8 39.1 %collective-permute-start.1 = (f32[56,128]{1,0:T(8,128)}, f32[56,128]{1,0:T(8,128)S(1)}, u32[]{:S(2)}, u32[]{:S(2)}) collective-permute-start(f32[56,128]{1,0:T(8,128)} %get-tuple-element.43), channel_id=1, source_target_pairs={{0,704},{64,128},{128,64},{192,256},{256,192},{320,384},{384,320},... | collective-permute-start | bytes 86024 | tf_op jit(solution)/shard_map/ppermute | solution.py:478
  25.3 26.6 %collective-permute-start.2 = (f32[56,128]{1,0:T(8,128)}, f32[56,128]{1,0:T(8,128)S(1)}, u32[]{:S(2)}, u32[]{:S(2)}) collective-permute-start(f32[56,128]{1,0:T(8,128)} %get-tuple-element.44), channel_id=1, source_target_pairs={{0,1},{1,0},{2,3},{3,2},{4,5},{5,4},{6,7},{7,6},{8,9},{9,8},{10,11... | collective-permute-start | bytes 86024 | tf_op jit(solution)/shard_map/ppermute | solution.py:478
  28.4 23.5 %collective-permute-start.3 = (f32[56,128]{1,0:T(8,128)}, f32[56,128]{1,0:T(8,128)S(1)}, u32[]{:S(2)}, u32[]{:S(2)}) collective-permute-start(f32[56,128]{1,0:T(8,128)} %get-tuple-element.45), channel_id=1, source_target_pairs={{0,63},{1,2},{2,1},{3,4},{4,3},{5,6},{6,5},{7,8},{8,7},{9,10},{10,... | collective-permute-start | bytes 86024 | tf_op jit(solution)/shard_map/ppermute | solution.py:478
  32.9 18.9 %all-to-all-start = ((f32[64,1,8]{2,1,0:T(1,128)}), f32[64,1,8]{2,1,0:T(1,128)S(1)}, u32[]{:S(2)}, u32[]{:S(2)}) async-start(f32[64,1,8]{2,1,0:T(1,128)} %bitcast.32), calls=%async_computation | async-start | bytes 65536 | tf_op jit(solution)/shard_map/all_to_all | solution.py:517
  51.9 0.6 copy-start
  51.9 0.6 copy-start.6
  51.9 0.6 copy-start.7
  51.9 0.6 copy-start.8
  51.9 0.6 copy-start.9
  61.9 14.1 %collective-permute-start.4 = (f32[56,128]{1,0:T(8,128)}, f32[56,128]{1,0:T(8,128)S(1)}, u32[]{:S(2)}, u32[]{:S(2)}) collective-permute-start(f32[56,128]{1,0:T(8,128)} %get-tuple-element.58), channel_id=1, source_target_pairs={{0,64},{64,0},{128,192},{192,128},{256,320},{320,256},{384,448},{4... | collective-permute-start | bytes 86024 | tf_op jit(solution)/shard_map/ppermute | solution.py:478
  63.8 12.2 %collective-permute-start.5 = (f32[56,128]{1,0:T(8,128)}, f32[56,128]{1,0:T(8,128)S(1)}, u32[]{:S(2)}, u32[]{:S(2)}) collective-permute-start(f32[56,128]{1,0:T(8,128)} %get-tuple-element.59), channel_id=1, source_target_pairs={{0,704},{64,128},{128,64},{192,256},{256,192},{320,384},{384,320},... | collective-permute-start | bytes 86024 | tf_op jit(solution)/shard_map/ppermute | solution.py:478
  66.7 9.4 %collective-permute-start.6 = (f32[56,128]{1,0:T(8,128)}, f32[56,128]{1,0:T(8,128)S(1)}, u32[]{:S(2)}, u32[]{:S(2)}) collective-permute-start(f32[56,128]{1,0:T(8,128)} %get-tuple-element.60), channel_id=1, source_target_pairs={{0,1},{1,0},{2,3},{3,2},{4,5},{5,4},{6,7},{7,6},{8,9},{9,8},{10,11... | collective-permute-start | bytes 86024 | tf_op jit(solution)/shard_map/ppermute | solution.py:478
  69.8 6.3 %collective-permute-start.7 = (f32[56,128]{1,0:T(8,128)}, f32[56,128]{1,0:T(8,128)S(1)}, u32[]{:S(2)}, u32[]{:S(2)}) collective-permute-start(f32[56,128]{1,0:T(8,128)} %get-tuple-element.61), channel_id=1, source_target_pairs={{0,63},{1,2},{2,1},{3,4},{4,3},{5,6},{6,5},{7,8},{8,7},{9,10},{10,... | collective-permute-start | bytes 86024 | tf_op jit(solution)/shard_map/ppermute | solution.py:478
  76.0 0.6 copy-start.2
  76.0 0.6 copy-start.3
  76.1 0.6 copy-start.4
  76.1 0.6 copy-start.5
  79.3 16.0 %all-to-all-start.1 = ((f32[64,1,8]{2,1,0:T(1,128)}), f32[64,1,8]{2,1,0:T(1,128)S(1)}, u32[]{:S(2)}, u32[]{:S(2)}) async-start(f32[64,1,8]{2,1,0:T(1,128)} %bitcast.35), calls=%async_computation.1 | async-start | bytes 65536 | tf_op jit(solution)/shard_map/all_to_all | solution.py:550
  95.3 0.6 copy-start.1
where the time goes:
time: 97.9 us; the launch traced here: 97.3 us
  starting transfers between devices  49.8 us (51%)
  Pallas kernels  33.3 us (34%)
  waiting for transfers between devices  11.5 us (12%)
  local copies, waits for them, and re-layouts  1.83 us (2%)
    ppermute x8, starting transfers between devices, pair_up(): return lax.ppermute(x, axis, pairs)  33.6 us
    all_to_all x1, starting transfers between devices, local(): params = lax.all_to_all(params, 'gy', 0, 0, tiled=True)  9.6 us
    pallas_call x1, Pallas kernels, local(): call(middle_kernel, [shape(FIELD), shape(FIELD), shape(TRACE), shape(TABL...  9.37 us
    pallas_call x1, Pallas kernels, local(): call(first_kernel, [shape(FIELD), shape(FIELD), shape(TRACE), shape(TABLE...  7.33 us
    all_to_all x1, starting transfers between devices, local(): back = lax.all_to_all(back, 'gy', 0, 0, tiled=True)  6.66 us
    all_to_all x1, waiting for transfers between devices, local(): back = lax.all_to_all(back, 'gy', 0, 0, tiled=True)  6.43 us
    all_to_all x1, waiting for transfers between devices, local(): params = lax.all_to_all(params, 'gy', 0, 0, tiled=True)  5.04 us
    pallas_call x1, Pallas kernels, local(): call(near_first_kernel, [shape(FIELD), shape(TRACE), shape(TABLE), shape(...  4.27 us
  transfers between devices with their start and end apart: 10, of which 2 were waited for; matrix products, arithmetic and copies ran while one was open for 0% of the time, Pallas kernels for 13%

commit v1 on v0

--- a/solution.py
+++ b/solution.py
@@ -4,6 +4,7 @@
 from jax.experimental import pallas as pl
 from jax.experimental.pallas import tpu as pltpu
 from jax.sharding import PartitionSpec as P
+
 
 F32 = jnp.float32
 BF16 = jnp.bfloat16
@@ -18,6 +19,7 @@
 PTS = 24
 ROWS = 224
 MSG = ROWS // 4
+LIMIT = 16 * 1024 * 1024
 WIDE = VARS * E
 
 
@@ -52,7 +54,7 @@
 def stack_stiffness(stiff_ref, tall_ref):
     tall_ref[...] = jnp.zeros_like(tall_ref)
     for d in range(3):
-        tall_ref[MODES * d : MODES * (d + 1), 0:MODES] = stiff_ref[d]
+        tall_ref[MODES * d : MODES * (d + 1), 0:MODES] = -stiff_ref[d]
     return widen(tall_ref[...])
 
 
@@ -71,61 +73,53 @@
             square_ref[PTS * f + j : PTS * f + j + 1, 0:MODES] = face_ref[j, f : f + 1, :]
 
 
-def load_rhs(read, rhs_ref):
+PAIRS = ((0, 1), (2, 3), (4, 5), (6, 7), (8,))
+
+
+def right_operand(fields):
     pad = jnp.zeros((64 - MODES, E), F32)
-    for w in range(VARS):
-        x = read(w)
+    columns = []
+    for x in fields:
         top = x.astype(BF16).astype(F32)
         high = jnp.concatenate([top, pad], axis=0).astype(BF16)
         low = jnp.concatenate([x - top, pad], axis=0).astype(BF16)
-        rhs_ref[0:64, lanes(w)] = high
-        rhs_ref[64:128, lanes(w)] = low
-        rhs_ref[128:192, lanes(w)] = high
-        rhs_ref[192:256, lanes(w)] = low
-
-
-def product(a, rhs_ref, out_ref):
-    for start in range(0, WIDE, 256):
-        cols = slice(start, min(start + 256, WIDE))
-        out_ref[:, cols] = dot(a, rhs_ref[:, cols])
-
-
-def star_mix(star_ref, tall_ref, emit):
-    def body(group, carry):
-        sums = [jnp.zeros((MODES, E), F32) for _ in range(3)]
-        for w in range(VARS):
-            for d in range(3):
-                x = tall_ref[MODES * d : MODES * (d + 1), lanes(w)]
-                for i in range(3):
-                    sums[i] = sums[i] + star_ref[3 * group + i, w, d : d + 1, :] * x
-        for i in range(3):
-            emit(3 * group + i, sums[i])
-        return carry
-
-    lax.fori_loop(0, 3, body, 0)
-
-
-def predict(start_ref, star_ref, left, deriv_ref, rhs_ref, tall_ref, early_ref, late_ref):
-    early_ref[...] = start_ref[...]
-    if late_ref is not None:
-        late_ref[...] = start_ref[...]
+        columns.append(jnp.concatenate([high, low, high, low], axis=0))
+    return jnp.concatenate(columns, axis=1)
+
+
+def product_of(left, read, out_ref):
+    for pair in PAIRS:
+        cols = slice(E * pair[0], E * (pair[-1] + 1))
+        out_ref[:, cols] = dot(left, right_operand([read(w) for w in pair]))
+
+
+def star_mix(star_ref, tall_ref, pair):
+    sums = [None] * len(pair)
+    for w in range(VARS):
+        for d in range(3):
+            x = tall_ref[MODES * d : MODES * (d + 1), lanes(w)]
+            for i, v in enumerate(pair):
+                term = star_ref[v, w, d : d + 1, :] * x
+                sums[i] = term if sums[i] is None else sums[i] + term
+    return sums
+
+
+def predict(start_ref, star_ref, left, tall_refs, early_ref, late_ref):
+    product_of(left, lambda w: start_ref[w], tall_refs[0])
     factor = 1.0
     for power in range(2, ORDER + 1):
         factor = factor * power
-        source = start_ref if power == 2 else deriv_ref
-        load_rhs(lambda w: source[w], rhs_ref)
-        product(left, rhs_ref, tall_ref)
-        to_early = 1.0 / factor
-        to_late = (2.0**power - 1.0) / factor
-
-        def emit(v, change):
+        source, target = tall_refs[power % 2], tall_refs[(power + 1) % 2]
+        for pair in PAIRS:
+            derivs = star_mix(star_ref, source, pair)
+            for v, deriv in zip(pair, derivs):
+                for out_ref, scale in ((early_ref, 1.0 / factor), (late_ref, (2.0**power - 1.0) / factor)):
+                    if out_ref is not None:
+                        base = start_ref[v] if power == 2 else out_ref[v]
+                        out_ref[v] = base + deriv * scale
             if power < ORDER:
-                deriv_ref[v] = -change
-            early_ref[v] = early_ref[v] - change * to_early
-            if late_ref is not None:
-                late_ref[v] = late_ref[v] - change * to_late
-
-        star_mix(star_ref, tall_ref, emit)
+                cols = slice(E * pair[0], E * (pair[-1] + 1))
+                target[:, cols] = dot(left, right_operand(derivs))
 
 
 def direction_rows(send_ref):
@@ -138,9 +132,8 @@
     return order
 
 
-def make_traces(left, integral_ref, rhs_ref, own_ref, table_ref, high_ref, low_ref):
-    load_rhs(lambda w: integral_ref[w], rhs_ref)
-    product(left, rhs_ref, own_ref)
+def make_traces(left, integral_ref, own_ref, table_ref, high_ref, low_ref):
+    product_of(left, lambda w: integral_ref[w], own_ref)
     for w in range(VARS):
         for f in range(FACES):
             table_ref[PTS * w : PTS * (w + 1), lanes(f)] = own_ref[PTS * f : PTS * (f + 1), lanes(w)]
@@ -321,27 +314,36 @@
 
 
 def first_kernel(
-    wave_ref, star_ref, stiff_ref, proj_ref, send_ref,
-    early_ref, late_ref, own_ref, high_ref, low_ref, m0, m1, m2, m3, ap_ref, at_ref,
-    deriv_ref, rhs_ref, tall_ref, lhs_ref, square_ref, table_ref,
-):
+    stiff_hbm, wave_hbm, star_hbm, proj_hbm, send_hbm, source_hbm, faces_hbm, owner_hbm, cluster_hbm, yield_hbm, mask_hbm,
+    send_ref, source_ref, faces_ref, owner_ref, cluster_ref, yield_ref, mask_ref, early_ref, late_ref, own_ref, high_ref, low_ref, m0, m1, m2, m3, ap_ref, at_ref,
+    tall_a, tall_b, lhs_ref, square_ref, table_ref,
+    stiff_ref, wave_ref, star_ref, proj_ref, *sems,
+):
+    sources = (stiff_hbm, wave_hbm, star_hbm, proj_hbm, send_hbm, source_hbm, faces_hbm, owner_hbm, cluster_hbm, yield_hbm, mask_hbm)
+    targets = (stiff_ref, wave_ref, star_ref, proj_ref, send_ref, source_ref, faces_ref, owner_ref, cluster_ref, yield_ref, mask_ref)
+    copies = [pltpu.make_async_copy(*each) for each in zip(sources, targets, sems)]
+    for copy in copies:
+        copy.start()
+    copies[0].wait()
     ap_ref[...] = stack_stiffness(stiff_ref, lhs_ref)
+    copies[3].wait()
     spread_faces(proj_ref, square_ref)
     at_ref[...] = widen(square_ref[0 : FACES * PTS])
-    predict(wave_ref, star_ref, ap_ref[...], deriv_ref, rhs_ref, tall_ref, early_ref, late_ref)
-    make_traces(at_ref[...], early_ref, rhs_ref, own_ref, table_ref, high_ref, low_ref)
+    copies[1].wait()
+    copies[2].wait()
+    for copy in copies[4:]:
+        copy.wait()
+    predict(wave_ref, star_ref, ap_ref[...], (tall_a, tall_b), early_ref, late_ref)
+    make_traces(at_ref[...], early_ref, own_ref, table_ref, high_ref, low_ref)
     make_messages(send_ref, high_ref, low_ref, (m0, m1, m2, m3))
 
 
 def near_work(integral_ref, star_ref, own_mats_ref, own_ref, high_ref, low_ref, source_ref, left,
-              vol_ref, flux_ref, near_ref, rhs_ref, tall_ref):
-    load_rhs(lambda w: integral_ref[w], rhs_ref)
-    product(left, rhs_ref, tall_ref)
-
-    def emit(v, total):
-        vol_ref[v] = total
-
-    star_mix(star_ref, tall_ref, emit)
+              vol_ref, flux_ref, near_ref, tall_ref):
+    product_of(left, lambda w: integral_ref[w], tall_ref)
+    for pair in PAIRS:
+        for v, total in zip(pair, star_mix(star_ref, tall_ref, pair)):
+            vol_ref[v] = total
     mix_faces(own_mats_ref, lambda f, w: own_ref[PTS * f : PTS * (f + 1), lanes(w)], None, flux_ref)
     for f in range(FACES):
         pick = one_hot(iota((FACES * E, E), 0) == source_ref[f : f + 1, :])
@@ -351,7 +353,7 @@
 def near_first_kernel(
     integral_ref, star_ref, own_mats_ref, own_ref, high_ref, low_ref, source_ref, stiff_ref, lift_ref,
     vol_ref, flux_ref, near_ref, av_ref, al_ref,
-    rhs_ref, tall_ref, lhs_ref, square_ref,
+    tall_ref, lhs_ref, square_ref,
 ):
     av_ref[...] = stack_stiffness_t(stiff_ref, lhs_ref, square_ref)
     spread_faces(lift_ref, square_ref)
@@ -359,23 +361,23 @@
     al_ref[0] = high
     al_ref[1] = low
     near_work(integral_ref, star_ref, own_mats_ref, own_ref, high_ref, low_ref, source_ref, av_ref[...],
-              vol_ref, flux_ref, near_ref, rhs_ref, tall_ref)
+              vol_ref, flux_ref, near_ref, tall_ref)
 
 
 def near_second_kernel(
     integral_ref, star_ref, own_mats_ref, own_ref, high_ref, low_ref, source_ref, av_ref,
     vol_ref, flux_ref, near_ref,
-    rhs_ref, tall_ref,
+    tall_ref,
 ):
     near_work(integral_ref, star_ref, own_mats_ref, own_ref, high_ref, low_ref, source_ref, av_ref[...],
-              vol_ref, flux_ref, near_ref, rhs_ref, tall_ref)
+              vol_ref, flux_ref, near_ref, tall_ref)
 
 
 def middle_kernel(
     wave_ref, late_ref, vol_ref, part_ref, near_ref, own_ref, m0, m1, m2, m3, nbr_mats_ref, source_ref,
     faces_ref, owner_ref, params_ref, star_ref, ap_ref, at_ref, al_ref, send_ref, cluster_ref, yield_ref, mask_ref,
     integral_ref, base_ref, own2_ref, high_ref, low_ref, n0, n1, n2, n3, par_ref,
-    nbr_ref, state_ref, flux_ref, lifted_ref, mid_ref, deriv_ref, rhs_ref, tall_ref, table_ref,
+    nbr_ref, state_ref, flux_ref, lifted_ref, mid_ref, tall_a, tall_b, table_ref,
 ):
     finish_gather(source_ref, (m0, m1, m2, m3), near_ref, nbr_ref)
     faces_row = faces_ref[...]
@@ -403,10 +405,10 @@
         midway = jnp.where(coarse, wave_ref[v], fine)
         mid_ref[v] = midway
         base_ref[v] = midway + base_ref[v]
-    predict(mid_ref, star_ref, ap_ref[...], deriv_ref, rhs_ref, tall_ref, integral_ref, None)
+    predict(mid_ref, star_ref, ap_ref[...], (tall_a, tall_b), integral_ref, None)
     for v in range(VARS):
         integral_ref[v] = jnp.where(coarse, late_ref[v], integral_ref[v])
-    make_traces(at_ref[...], integral_ref, rhs_ref, own2_ref, table_ref, high_ref, low_ref)
+    make_traces(at_ref[...], integral_ref, own2_ref, table_ref, high_ref, low_ref)
     make_messages(send_ref, high_ref, low_ref, (n0, n1, n2, n3))
 
 
@@ -453,12 +455,22 @@
     return jax.ShapeDtypeStruct(dims, dtype)
 
 
-def call(kernel, outs, scratch=()):
-    return pl.pallas_call(
-        kernel,
-        out_shape=outs,
-        scratch_shapes=[pltpu.VMEM(dims, dtype) for dims, dtype in scratch],
-    )
+def call(kernel, outs, scratch=(), hbm=0):
+    in_vmem = pl.BlockSpec(memory_space=pltpu.VMEM)
+    in_hbm = pl.BlockSpec(memory_space=pltpu.HBM)
+    many = isinstance(outs, list)
+
+    def run(*args):
+        return pl.pallas_call(
+            kernel,
+            out_shape=outs,
+            in_specs=[in_hbm] * hbm + [in_vmem] * (len(args) - hbm),
+            out_specs=[in_vmem] * len(outs) if many else in_vmem,
+            scratch_shapes=[pltpu.VMEM(dims, dtype) for dims, dtype in scratch] + [pltpu.SemaphoreType.DMA] * hbm,
+            compiler_params=pltpu.CompilerParams(vmem_limit_bytes=LIMIT),
+        )(*args)
+
+    return run
 
 
 FIELD = (VARS, MODES, E)
@@ -466,7 +478,6 @@
 TABLE = (ROWS, FACES * E)
 LEFT = (3 * MODES, 256)
 TALL = (3 * MODES, WIDE)
-RHS = (256, WIDE)
 
 
 def pair_up(x, axis, odd):
@@ -478,8 +489,14 @@
     return lax.ppermute(x, axis, pairs)
 
 
+EDGES = (("gx", 0), ("gx", 1), ("gy", 0), ("gy", 1))
+
+
 def exchange(messages):
-    return [pair_up(x, axis, odd) for x, (axis, odd) in zip(messages, (("gx", 0), ("gx", 1), ("gy", 0), ("gy", 1)))]
+    received = []
+    for x, (axis, odd) in zip(messages, EDGES):
+        received.append(pair_up(x, axis, odd))
+    return received
 
 
 def local(
@@ -517,13 +534,19 @@
     params = lax.all_to_all(params, "gy", 0, 0, tiled=True)
 
     messages = [shape((MSG, E))] * 4
-    work = [(FIELD, F32), (RHS, BF16), (TALL, F32)]
-    early, late, own, high, low, m0, m1, m2, m3, ap, at = call(
+    small = (send_faces, face_source, fault_faces, owner, cluster, yield_stress, plastic_mask)
+    firsts = [pltpu.with_memory_space_constraint(x, pltpu.HBM) for x in (stiffness, wavefield, star, proj, *small)]
+    work = [(TALL, F32), (TALL, F32)]
+    (send_faces, face_source, fault_faces, owner, cluster, yield_stress, plastic_mask,
+     early, late, own, high, low, m0, m1, m2, m3, ap, at) = call(
         first_kernel,
-        [shape(FIELD), shape(FIELD), shape(TRACE), shape(TABLE, BF16), shape(TABLE, BF16), *messages,
+        [*(shape(x.shape, x.dtype) for x in small),
+         shape(FIELD), shape(FIELD), shape(TRACE), shape(TABLE, BF16), shape(TABLE, BF16), *messages,
          shape(LEFT, BF16), shape((FACES * PTS, 256), BF16)],
-        work + [((3 * MODES, E), F32), ((E, E), F32), (TABLE, F32)],
-    )(wavefield, star, stiffness, proj, send_faces)
+        work + [((3 * MODES, E), F32), ((E, E), F32), (TABLE, F32)]
+        + [(x.shape, x.dtype) for x in firsts[0:4]],
+        hbm=len(firsts),
+    )(*firsts)
     got = exchange((m0, m1, m2, m3))
     vol, part, near, av, al = call(
         near_first_kernel,
@@ -558,6 +581,7 @@
 def solution(mesh):
     flat = ("gx", "gy")
     last2, last3, last1 = P(None, None, flat), P(None, None, None, flat), P(flat)
+
     return jax.shard_map(
         local,
         mesh=mesh,

time: 97.9 us -> 91.6 us (0.936)
  Pallas kernels: 33.3 us -> 20.4 us
  waiting for transfers between devices: 11.5 us -> 14.8 us
  local copies, waits for them, and re-layouts: 1.83 us -> 4.16 us
    pallas_call x8, Pallas kernels: 33.3 us -> 20.4 us  [run(): pl.pallas_call(kernel, out_shape=outs, in_specs=[in_hbm] * hbm + [in_vmem...]
    unnamed x20 -> x34, local copies, waits for them, and re-layouts: 1.83 us -> 4.16 us
    all_to_all x1, waiting for transfers between devices: 6.43 us -> 7.97 us  [local(): back = lax.all_to_all(back, 'gy', 0, 0, tiled=True)]
  transfers between devices with their start and end apart: 10 -> 10, of which waited for: 2 -> 3; matrix products, arithmetic and copies ran while one was open for 0% -> 0% of each run, Pallas kernels for 13% -> 7%
where the time goes in v1:
time: 91.6 us; the launch traced here: 91 us
  starting transfers between devices  50.7 us (55%)
  Pallas kernels  20.4 us (22%)
  waiting for transfers between devices  14.8 us (16%)
  local copies, waits for them, and re-layouts  4.16 us (5%)
  between operations  0.94 us (1%)
    ppermute x8, starting transfers between devices, pair_up(): return lax.ppermute(x, axis, pairs)  33.7 us
    pallas_call x8, Pallas kernels, run(): pl.pallas_call(kernel, out_shape=outs, in_specs=[in_hbm] * hbm + [in_vmem...  20.4 us
    all_to_all x1, starting transfers between devices, local(): params = lax.all_to_all(params, 'gy', 0, 0, tiled=True)  9.6 us
    all_to_all x1, waiting for transfers between devices, local(): back = lax.all_to_all(back, 'gy', 0, 0, tiled=True)  7.97 us
    all_to_all x1, starting transfers between devices, local(): back = lax.all_to_all(back, 'gy', 0, 0, tiled=True)  7.36 us
    all_to_all x1, waiting for transfers between devices, local(): params = lax.all_to_all(params, 'gy', 0, 0, tiled=True)  5.83 us
    unnamed x34, local copies, waits for them, and re-layouts  4.16 us
  transfers between devices with their start and end apart: 10, of which 3 were waited for; matrix products, arithmetic and copies ran while one was open for 0% of the time, Pallas kernels for 7%

profile of v1, /device:TPU:1, one launch (start us, length us, event | category | flops | bytes accessed | tf_op | source)
XLA Modules:
  0.0 91.0 jit_solution(13914659364428983481)
XLA Ops:
  0.6 0.0 copy-start.12
  0.6 0.0 copy-start.13
  0.7 0.0 copy-start.14
  0.7 0.0 copy-start
  0.7 0.0 copy-start.2
  0.7 6.1 %shard_map.176 = (s32[4,32]{1,0:T(4,128)S(1)}, s32[4,128]{1,0:T(4,128)S(1)}, s32[1,64]{1,0:T(1,128)S(1)}, s32[1,64]{1,0:T(1,128)S(1)}, s32[1,128]{1,0:T(1,128)S(...) custom-call(f32[3,56,56]{2,1,0:T(8,128)} %stiff_ref.1, ...), custom_call_target="tpu_custom_call" | custom-call | tf_op jit(solution)/shard_map/pallas_call | solution.py:464
  6.8 0.0 copy-start.7
  6.8 0.6 copy-done.7
  7.4 0.0 copy-start.10
  7.4 0.0 copy-start.15
  7.4 0.0 copy-start.4
  7.4 0.6 copy-done.10
  8.0 0.0 copy-done.15
  8.0 4.8 %collective-permute-start = (f32[56,128]{1,0:T(8,128)}, f32[56,128]{1,0:T(8,128)}, u32[]{:S(2)}, u32[]{:S(2)}) collective-permute-start(f32[56,128]{1,0:T(8,128)} %get-tuple-element.50), channel_id=1, source_target_pairs={{0,64},{64,0},{128,192},{192,128},{256,320},{320,256},{384,448},{4... | collective-permute-start | bytes 86024 | tf_op jit(solution)/shard_map/ppermute | solution.py:489
  12.8 12.5 %collective-permute-start.1 = (f32[56,128]{1,0:T(8,128)}, f32[56,128]{1,0:T(8,128)}, u32[]{:S(2)}, u32[]{:S(2)}) collective-permute-start(f32[56,128]{1,0:T(8,128)} %get-tuple-element.51), channel_id=1, source_target_pairs={{0,704},{64,128},{128,64},{192,256},{256,192},{320,384},{384,320},... | collective-permute-start | bytes 86024 | tf_op jit(solution)/shard_map/ppermute | solution.py:489
  25.3 3.1 %collective-permute-start.2 = (f32[56,128]{1,0:T(8,128)}, f32[56,128]{1,0:T(8,128)}, u32[]{:S(2)}, u32[]{:S(2)}) collective-permute-start(f32[56,128]{1,0:T(8,128)} %get-tuple-element.52), channel_id=1, source_target_pairs={{0,1},{1,0},{2,3},{3,2},{4,5},{5,4},{6,7},{7,6},{8,9},{9,8},{10,11... | collective-permute-start | bytes 86024 | tf_op jit(solution)/shard_map/ppermute | solution.py:489
  28.4 3.1 %collective-permute-start.3 = (f32[56,128]{1,0:T(8,128)}, f32[56,128]{1,0:T(8,128)}, u32[]{:S(2)}, u32[]{:S(2)}) collective-permute-start(f32[56,128]{1,0:T(8,128)} %get-tuple-element.53), channel_id=1, source_target_pairs={{0,63},{1,2},{2,1},{3,4},{4,3},{5,6},{6,5},{7,8},{8,7},{9,10},{10,... | collective-permute-start | bytes 86024 | tf_op jit(solution)/shard_map/ppermute | solution.py:489
  31.5 0.0 copy-done.12
  31.6 0.0 copy-done.13
  31.6 0.0 copy-done.14
  31.6 0.7 shard_map.178
  32.3 9.6 %all-to-all-start = ((f32[64,1,8]{2,1,0:T(1,128)}), f32[64,1,8]{2,1,0:T(1,128)S(1)}, u32[]{:S(2)}, u32[]{:S(2)}) async-start(f32[64,1,8]{2,1,0:T(1,128)} %bitcast.13), calls=%async_computation | async-start | bytes 65536 | tf_op jit(solution)/shard_map/all_to_all | solution.py:534
  41.9 0.0 copy-done
  41.9 0.0 copy-done.2
  41.9 0.0 copy-done.4
  41.9 0.0 copy-start.9
  42.0 0.8 copy-done.9
  42.7 0.0 copy-start.1
  42.7 0.0 copy-start.3
  42.7 2.0 %shard_map.177 = (f32[9,56,128]{2,1,0:T(8,128)S(1)}, f32[96,1152]{1,0:T(8,128)S(1)}, f32[224,512]{1,0:T(8,128)S(1)}, bf16[168,256]{1,0:T(8,128)(2,1)S(1)}, bf16[2,56,128]{2,1,0:T(8,128)(2,1)S(1)}) custom-call(f32[9,56,128]{2,1,0:T(8,128)S(1)} %get-tuple-element.42.integral_ref, f32[9,9,3,128]{3,2,1,0:T(4,128)S(1)} %bitcast.22, ...), custom_call_target="tpu_custom_call" | custom-call | tf_op jit(solution)/shard_map/pallas_call | solution.py:464
  44.8 0.0 copy-start.5
  44.8 0.6 copy-done.5
  45.4 5.8 %all-to-all-done = f32[64,1,8]{2,1,0:T(1,128)S(1)} async-done(((f32[64,1,8]{2,1,0:T(1,128)}), f32[64,1,8]{2,1,0:T(1,128)S(1)}, u32[]{:S(2)}, u32[]{:S(2)}) %all-to-all-start) | async-done | bytes 2080 | tf_op jit(solution)/shard_map/all_to_all | solution.py:534
  51.2 0.0 collective-permute-done.m0
  51.2 0.0 collective-permute-done.1.m1
  51.2 0.0 collective-permute-done.2.m2
  51.2 0.0 collective-permute-done.3.m3
  51.2 0.0 copy-start.11
  51.3 0.0 copy-start.16
  51.3 0.0 copy-done.1
  51.3 0.0 copy-done.3
  51.3 0.6 copy-done.11
  51.9 0.0 copy-done.16
  51.9 0.0 copy-start.8
  51.9 0.9 copy-done.8
  52.8 0.0 copy-start.6
  52.8 6.3 %shard_map.179 = (f32[9,56,128]{2,1,0:T(8,128)S(1)}, f32[9,56,128]{2,1,0:T(8,128)S(1)}, f32[96,1152]{1,0:T(8,128)S(1)}, bf16[224,512]{1,0:T(8,128)(2,1)S(1)}, bf...) custom-call(f32[9,56,128]{2,1,0:T(8,128)S(1)} %copy-done.1, ...), custom_call_target="tpu_custom_call" | custom-call | tf_op jit(solution)/shard_map/pallas_call | solution.py:464
  59.1 1.9 %collective-permute-start.4 = (f32[56,128]{1,0:T(8,128)S(1)}, f32[56,128]{1,0:T(8,128)S(1)}, u32[]{:S(2)}, u32[]{:S(2)}) collective-permute-start(f32[56,128]{1,0:T(8,128)S(1)} %get-tuple-element.72), channel_id=1, source_target_pairs={{0,64},{64,0},{128,192},{192,128},{256,320},{320,256},{384,448},{4... | collective-permute-start | bytes 86024 | tf_op jit(solution)/shard_map/ppermute | solution.py:489
  61.0 2.8 %collective-permute-start.5 = (f32[56,128]{1,0:T(8,128)S(1)}, f32[56,128]{1,0:T(8,128)S(1)}, u32[]{:S(2)}, u32[]{:S(2)}) collective-permute-start(f32[56,128]{1,0:T(8,128)S(1)} %get-tuple-element.73), channel_id=1, source_target_pairs={{0,704},{64,128},{128,64},{192,256},{256,192},{320,384},{384,320},... | collective-permute-start | bytes 86024 | tf_op jit(solution)/shard_map/ppermute | solution.py:489
  63.9 3.1 %collective-permute-start.6 = (f32[56,128]{1,0:T(8,128)S(1)}, f32[56,128]{1,0:T(8,128)S(1)}, u32[]{:S(2)}, u32[]{:S(2)}) collective-permute-start(f32[56,128]{1,0:T(8,128)S(1)} %get-tuple-element.74), channel_id=1, source_target_pairs={{0,1},{1,0},{2,3},{3,2},{4,5},{5,4},{6,7},{7,6},{8,9},{9,8},{10,11... | collective-permute-start | bytes 86024 | tf_op jit(solution)/shard_map/ppermute | solution.py:489
  67.0 2.3 %collective-permute-start.7 = (f32[56,128]{1,0:T(8,128)S(1)}, f32[56,128]{1,0:T(8,128)S(1)}, u32[]{:S(2)}, u32[]{:S(2)}) collective-permute-start(f32[56,128]{1,0:T(8,128)S(1)} %get-tuple-element.75), channel_id=1, source_target_pairs={{0,63},{1,2},{2,1},{3,4},{4,3},{5,6},{6,5},{7,8},{8,7},{9,10},{10,... | collective-permute-start | bytes 86024 | tf_op jit(solution)/shard_map/ppermute | solution.py:489
  69.4 0.0 copy-done.6
  69.4 1.8 %shard_map.180 = (f32[9,56,128]{2,1,0:T(8,128)S(1)}, f32[96,1152]{1,0:T(8,128)S(1)}, f32[224,512]{1,0:T(8,128)S(1)}) custom-call(f32[9,56,128]{2,1,0:T(8,128)S(1)} %get-tuple-element.64.integral_ref, f32[9,9,3,128]{3,2,1,0:T(4,128)S(1)} %bitcast.24, f32[9,9,4,128]{3,2,1,0:T(4,128)S(1)} %bitcast.26, f32[96,1152]{1,0:T(8,128)S(1)} %get-tuple-element.65.own_ref, ...), custom_call_target="tpu_custom_call" | custom-call | tf_op jit(solution)/shard_map/pallas_call | solution.py:464
  71.2 0.0 collective-permute-done.4.m0
  71.2 0.0 collective-permute-done.5.m1
  71.2 0.0 collective-permute-done.6.m2
  71.2 1.0 %collective-permute-done.7.m3 = f32[56,128]{1,0:T(8,128)S(1)} collective-permute-done((f32[56,128]{1,0:T(8,128)S(1)}, f32[56,128]{1,0:T(8,128)S(1)}, u32[]{:S(2)}, u32[]{:S(2)}) %collective-permute-start.7) | collective-permute-done | bytes 28704 | tf_op jit(solution)/shard_map/ppermute | solution.py:489
  72.2 1.4 %shard_map.181 = (f32[224,512]{1,0:T(8,128)S(1)}, f32[48,512]{1,0:T(8,128)S(1)}, f32[64,8]{1,0:T(8,128)}) custom-call(f32[224,512]{1,0:T(8,128)S(1)} %get-tuple-element.71.near_ref, f32[96,1152]{1,0:T(8,128)S(1)} %get-tuple-element.65.own_ref, f32[56,128]{1,0:T(8,128)S(1)} %collective-permute-done.4.m0, f32[56,128]{1,0:T(8,128)S(1)} %collective-permute-done.5.m1, ...), custom_call_target="tpu_custom_call" | custom-call | tf_op jit(solution)/shard_map/pallas_call | solution.py:464
  73.6 7.4 %all-to-all-start.1 = ((f32[64,1,8]{2,1,0:T(1,128)}), f32[64,1,8]{2,1,0:T(1,128)S(1)}, u32[]{:S(2)}, u32[]{:S(2)}) async-start(f32[64,1,8]{2,1,0:T(1,128)} %bitcast.16), calls=%async_computation.1 | async-start | bytes 65536 | tf_op jit(solution)/shard_map/all_to_all | solution.py:573
  80.9 1.5 %shard_map.182 = f32[9,56,128]{2,1,0:T(8,128)} custom-call(f32[9,56,128]{2,1,0:T(8,128)S(1)} %get-tuple-element.63.base_ref, f32[9,56,128]{2,1,0:T(8,128)S(1)} %get-tuple-element.69.vol_ref, f32[96,1152]{1,0:T(8,128)S(1)} %get-tuple-element.70.part_ref, f32[224,512]{1,0:T(8,128)S(1)} %get-tuple-element.77.nbr_ref, ...), custom_call_target="tpu_custom_call" | custom-call | tf_op jit(solution)/shard_map/pallas_call | solution.py:464
  82.4 8.0 %all-to-all-done.1 = f32[64,1,8]{2,1,0:T(1,128)S(1)} async-done(((f32[64,1,8]{2,1,0:T(1,128)}), f32[64,1,8]{2,1,0:T(1,128)S(1)}, u32[]{:S(2)}, u32[]{:S(2)}) %all-to-all-start.1) | async-done | bytes 2080 | tf_op jit(solution)/shard_map/all_to_all | solution.py:573
  90.4 0.6 shard_map.183
Async XLA Ops:
  0.6 30.9 %copy-start.12 = (f32[128]{0:T(128)S(1)}, f32[128]{0:T(128)}, u32[]{:S(2)}) copy-start(f32[128]{0:T(128)} %param.31) | copy-start | bytes 1540
  0.6 30.9 %copy-start.13 = (f32[128]{0:T(128)S(1)}, f32[128]{0:T(128)}, u32[]{:S(2)}) copy-start(f32[128]{0:T(128)} %param.32) | copy-start | bytes 1540
  0.7 30.9 %copy-start.14 = (s32[128]{0:T(128)S(1)}, s32[128]{0:T(128)}, u32[]{:S(2)}) copy-start(s32[128]{0:T(128)} %param.33) | copy-start | bytes 1540
  0.7 41.2 %copy-start = (f32[3,9,9,128]{3,0,2,1:T(4,128)S(1)}, f32[3,9,9,128]{3,0,2,1:T(4,128)}, u32[]{:S(2)}) copy-start(f32[3,9,9,128]{3,0,2,1:T(4,128)} %param.18) | copy-start | bytes 373252
  0.7 41.2 %copy-start.2 = (f32[4,9,9,128]{3,0,2,1:T(4,128)S(1)}, f32[4,9,9,128]{3,0,2,1:T(4,128)}, u32[]{:S(2)}) copy-start(f32[4,9,9,128]{3,0,2,1:T(4,128)} %param.19) | copy-start | bytes 497668
  6.8 0.6 copy-start.7
  7.4 0.6 copy-start.10
  7.4 0.6 copy-start.15
  7.4 34.5 %copy-start.4 = (f32[3,56,56]{2,1,0:T(8,128)S(1)}, f32[3,56,56]{2,1,0:T(8,128)}, u32[]{:S(2)}) copy-start(f32[3,56,56]{2,1,0:T(8,128)} %stiff_ref.1) | copy-start | bytes 112900
  8.0 43.3 %collective-permute-start = (f32[56,128]{1,0:T(8,128)}, f32[56,128]{1,0:T(8,128)}, u32[]{:S(2)}, u32[]{:S(2)}) collective-permute-start(f32[56,128]{1,0:T(8,128)} %get-tuple-element.50), channel_id=1, source_target_pairs={{0,64},{64,0},{128,192},{192,128},{256,320},{320,256},{384,448},{4... | collective-permute-start | bytes 86024 | tf_op jit(solution)/shard_map/ppermute | solution.py:489
  12.8 38.4 %collective-permute-start.1 = (f32[56,128]{1,0:T(8,128)}, f32[56,128]{1,0:T(8,128)}, u32[]{:S(2)}, u32[]{:S(2)}) collective-permute-start(f32[56,128]{1,0:T(8,128)} %get-tuple-element.51), channel_id=1, source_target_pairs={{0,704},{64,128},{128,64},{192,256},{256,192},{320,384},{384,320},... | collective-permute-start | bytes 86024 | tf_op jit(solution)/shard_map/ppermute | solution.py:489
  25.3 26.0 %collective-permute-start.2 = (f32[56,128]{1,0:T(8,128)}, f32[56,128]{1,0:T(8,128)}, u32[]{:S(2)}, u32[]{:S(2)}) collective-permute-start(f32[56,128]{1,0:T(8,128)} %get-tuple-element.52), channel_id=1, source_target_pairs={{0,1},{1,0},{2,3},{3,2},{4,5},{5,4},{6,7},{7,6},{8,9},{9,8},{10,11... | collective-permute-start | bytes 86024 | tf_op jit(solution)/shard_map/ppermute | solution.py:489
  28.4 22.8 %collective-permute-start.3 = (f32[56,128]{1,0:T(8,128)}, f32[56,128]{1,0:T(8,128)}, u32[]{:S(2)}, u32[]{:S(2)}) collective-permute-start(f32[56,128]{1,0:T(8,128)} %get-tuple-element.53), channel_id=1, source_target_pairs={{0,63},{1,2},{2,1},{3,4},{4,3},{5,6},{6,5},{7,8},{8,7},{9,10},{10,... | collective-permute-start | bytes 86024 | tf_op jit(solution)/shard_map/ppermute | solution.py:489
  32.3 18.9 %all-to-all-start = ((f32[64,1,8]{2,1,0:T(1,128)}), f32[64,1,8]{2,1,0:T(1,128)S(1)}, u32[]{:S(2)}, u32[]{:S(2)}) async-start(f32[64,1,8]{2,1,0:T(1,128)} %bitcast.13), calls=%async_computation | async-start | bytes 65536 | tf_op jit(solution)/shard_map/all_to_all | solution.py:534
  41.9 0.8 copy-start.9
  42.7 8.5 %copy-start.1 = (f32[9,56,128]{2,1,0:T(8,128)S(1)}, f32[9,56,128]{2,1,0:T(8,128)}, u32[]{:S(2)}) copy-start(f32[9,56,128]{2,1,0:T(8,128)} %wave_ref.1) | copy-start | bytes 774148
  42.7 8.5 %copy-start.3 = (f32[4,9,9,128]{3,0,2,1:T(4,128)S(1)}, f32[4,9,9,128]{3,0,2,1:T(4,128)}, u32[]{:S(2)}) copy-start(f32[4,9,9,128]{3,0,2,1:T(4,128)} %param.20) | copy-start | bytes 497668
  44.8 0.6 copy-start.5
  51.2 0.7 copy-start.11
  51.3 0.7 copy-start.16
  51.9 0.9 copy-start.8
  52.8 16.6 %copy-start.6 = (bf16[168,256]{1,0:T(8,128)(2,1)S(1)}, bf16[168,256]{1,0:T(8,128)(2,1)}, u32[]{:S(2)}) copy-start(bf16[168,256]{1,0:T(8,128)(2,1)} %copy-done.5) | copy-start | bytes 258052
  59.1 12.1 %collective-permute-start.4 = (f32[56,128]{1,0:T(8,128)S(1)}, f32[56,128]{1,0:T(8,128)S(1)}, u32[]{:S(2)}, u32[]{:S(2)}) collective-permute-start(f32[56,128]{1,0:T(8,128)S(1)} %get-tuple-element.72), channel_id=1, source_target_pairs={{0,64},{64,0},{128,192},{192,128},{256,320},{320,256},{384,448},{4... | collective-permute-start | bytes 86024 | tf_op jit(solution)/shard_map/ppermute | solution.py:489
  61.0 10.2 %collective-permute-start.5 = (f32[56,128]{1,0:T(8,128)S(1)}, f32[56,128]{1,0:T(8,128)S(1)}, u32[]{:S(2)}, u32[]{:S(2)}) collective-permute-start(f32[56,128]{1,0:T(8,128)S(1)} %get-tuple-element.73), channel_id=1, source_target_pairs={{0,704},{64,128},{128,64},{192,256},{256,192},{320,384},{384,320},... | collective-permute-start | bytes 86024 | tf_op jit(solution)/shard_map/ppermute | solution.py:489
  63.9 7.3 %collective-permute-start.6 = (f32[56,128]{1,0:T(8,128)S(1)}, f32[56,128]{1,0:T(8,128)S(1)}, u32[]{:S(2)}, u32[]{:S(2)}) collective-permute-start(f32[56,128]{1,0:T(8,128)S(1)} %get-tuple-element.74), channel_id=1, source_target_pairs={{0,1},{1,0},{2,3},{3,2},{4,5},{5,4},{6,7},{7,6},{8,9},{9,8},{10,11... | collective-permute-start | bytes 86024 | tf_op jit(solution)/shard_map/ppermute | solution.py:489
  67.0 5.2 %collective-permute-start.7 = (f32[56,128]{1,0:T(8,128)S(1)}, f32[56,128]{1,0:T(8,128)S(1)}, u32[]{:S(2)}, u32[]{:S(2)}) collective-permute-start(f32[56,128]{1,0:T(8,128)S(1)} %get-tuple-element.75), channel_id=1, source_target_pairs={{0,63},{1,2},{2,1},{3,4},{4,3},{5,6},{6,5},{7,8},{8,7},{9,10},{10,... | collective-permute-start | bytes 86024 | tf_op jit(solution)/shard_map/ppermute | solution.py:489
  73.6 16.8 %all-to-all-start.1 = ((f32[64,1,8]{2,1,0:T(1,128)}), f32[64,1,8]{2,1,0:T(1,128)S(1)}, u32[]{:S(2)}, u32[]{:S(2)}) async-start(f32[64,1,8]{2,1,0:T(1,128)} %bitcast.16), calls=%async_computation.1 | async-start | bytes 65536 | tf_op jit(solution)/shard_map/all_to_all | solution.py:573

commit v2 on v1

--- a/solution.py
+++ b/solution.py
@@ -289,7 +289,15 @@
     return [mean + factor * x for x in dev] + [factor * x for x in q[3:6]]
 
 
-def params_kernel(slip_ref, cohesion_ref, flag_ref, out_ref):
+def params_kernel(count, *refs):
+    inputs, out_ref, passed = refs[0 : 3 + count], refs[3 + count], refs[4 + count : 4 + 2 * count]
+    slots, sems = refs[4 + 2 * count : 7 + 2 * count], refs[7 + 2 * count :]
+    copies = [pltpu.make_async_copy(*each) for each in zip(inputs, (*slots, *passed), sems)]
+    for copy in copies:
+        copy.start()
+    for copy in copies[0:3]:
+        copy.wait()
+    slip_ref, cohesion_ref, flag_ref = slots
     gy_size = out_ref.shape[0]
     shape = (gy_size, slip_ref.shape[1])
     cols = []
@@ -302,6 +310,8 @@
     for i, col in enumerate(cols):
         out = jnp.where(column == i, col, out)
     out_ref[...] = out
+    for copy in copies[3:]:
+        copy.wait()
 
 
 def slip_kernel(in_ref, out_ref):
@@ -314,25 +324,13 @@
 
 
 def first_kernel(
-    stiff_hbm, wave_hbm, star_hbm, proj_hbm, send_hbm, source_hbm, faces_hbm, owner_hbm, cluster_hbm, yield_hbm, mask_hbm,
-    send_ref, source_ref, faces_ref, owner_ref, cluster_ref, yield_ref, mask_ref, early_ref, late_ref, own_ref, high_ref, low_ref, m0, m1, m2, m3, ap_ref, at_ref,
+    stiff_ref, wave_ref, star_ref, proj_ref, send_ref,
+    early_ref, late_ref, own_ref, high_ref, low_ref, m0, m1, m2, m3, ap_ref, at_ref,
     tall_a, tall_b, lhs_ref, square_ref, table_ref,
-    stiff_ref, wave_ref, star_ref, proj_ref, *sems,
-):
-    sources = (stiff_hbm, wave_hbm, star_hbm, proj_hbm, send_hbm, source_hbm, faces_hbm, owner_hbm, cluster_hbm, yield_hbm, mask_hbm)
-    targets = (stiff_ref, wave_ref, star_ref, proj_ref, send_ref, source_ref, faces_ref, owner_ref, cluster_ref, yield_ref, mask_ref)
-    copies = [pltpu.make_async_copy(*each) for each in zip(sources, targets, sems)]
-    for copy in copies:
-        copy.start()
-    copies[0].wait()
+):
     ap_ref[...] = stack_stiffness(stiff_ref, lhs_ref)
-    copies[3].wait()
     spread_faces(proj_ref, square_ref)
     at_ref[...] = widen(square_ref[0 : FACES * PTS])
-    copies[1].wait()
-    copies[2].wait()
-    for copy in copies[4:]:
-        copy.wait()
     predict(wave_ref, star_ref, ap_ref[...], (tall_a, tall_b), early_ref, late_ref)
     make_traces(at_ref[...], early_ref, own_ref, table_ref, high_ref, low_ref)
     make_messages(send_ref, high_ref, low_ref, (m0, m1, m2, m3))
@@ -451,20 +449,24 @@
         out_ref[v] = stressed[v]
 
 
+def in_hbm(x):
+    return pltpu.with_memory_space_constraint(x, pltpu.HBM)
+
+
 def shape(dims, dtype=F32):
     return jax.ShapeDtypeStruct(dims, dtype)
 
 
 def call(kernel, outs, scratch=(), hbm=0):
     in_vmem = pl.BlockSpec(memory_space=pltpu.VMEM)
-    in_hbm = pl.BlockSpec(memory_space=pltpu.HBM)
+    from_hbm = pl.BlockSpec(memory_space=pltpu.HBM)
     many = isinstance(outs, list)
 
     def run(*args):
         return pl.pallas_call(
             kernel,
             out_shape=outs,
-            in_specs=[in_hbm] * hbm + [in_vmem] * (len(args) - hbm),
+            in_specs=[from_hbm] * hbm + [in_vmem] * (len(args) - hbm),
             out_specs=[in_vmem] * len(outs) if many else in_vmem,
             scratch_shapes=[pltpu.VMEM(dims, dtype) for dims, dtype in scratch] + [pltpu.SemaphoreType.DMA] * hbm,
             compiler_params=pltpu.CompilerParams(vmem_limit_bytes=LIMIT),
@@ -530,23 +532,26 @@
     cluster, yield_stress, plastic_mask = (x.reshape(1, E) for x in (cluster, yield_stress, plastic_mask))
     slots = [x.reshape(1, slot_count) for x in (fault_slip, cohesion, slip_flag)]
 
-    params = call(params_kernel, shape((gy_size, 8)))(*slots)
+    small = (send_faces, face_source, fault_faces, owner, cluster, yield_stress, plastic_mask)
+    firsts = (stiffness, wavefield, star, proj, *small)
+    params, *brought = call(
+        lambda *refs: params_kernel(len(firsts), *refs),
+        [shape((gy_size, 8)), *(shape(x.shape, x.dtype) for x in firsts)],
+        [(x.shape, x.dtype) for x in slots],
+        hbm=3 + len(firsts),
+    )(*(in_hbm(x) for x in (*slots, *firsts)))
+    stiffness, wavefield, star_first, proj = brought[0:4]
+    send_faces, face_source, fault_faces, owner, cluster, yield_stress, plastic_mask = brought[4:]
     params = lax.all_to_all(params, "gy", 0, 0, tiled=True)
 
     messages = [shape((MSG, E))] * 4
-    small = (send_faces, face_source, fault_faces, owner, cluster, yield_stress, plastic_mask)
-    firsts = [pltpu.with_memory_space_constraint(x, pltpu.HBM) for x in (stiffness, wavefield, star, proj, *small)]
     work = [(TALL, F32), (TALL, F32)]
-    (send_faces, face_source, fault_faces, owner, cluster, yield_stress, plastic_mask,
-     early, late, own, high, low, m0, m1, m2, m3, ap, at) = call(
+    early, late, own, high, low, m0, m1, m2, m3, ap, at = call(
         first_kernel,
-        [*(shape(x.shape, x.dtype) for x in small),
-         shape(FIELD), shape(FIELD), shape(TRACE), shape(TABLE, BF16), shape(TABLE, BF16), *messages,
+        [shape(FIELD), shape(FIELD), shape(TRACE), shape(TABLE, BF16), shape(TABLE, BF16), *messages,
          shape(LEFT, BF16), shape((FACES * PTS, 256), BF16)],
-        work + [((3 * MODES, E), F32), ((E, E), F32), (TABLE, F32)]
-        + [(x.shape, x.dtype) for x in firsts[0:4]],
-        hbm=len(firsts),
-    )(*firsts)
+        work + [((3 * MODES, E), F32), ((E, E), F32), (TABLE, F32)],
+    )(stiffness, wavefield, star_first, proj, send_faces)
     got = exchange((m0, m1, m2, m3))
     vol, part, near, av, al = call(
         near_first_kernel,

time: 91.6 us -> 91.5 us (level)
    unnamed x34 -> x24, local copies, waits for them, and re-layouts: 4.16 us -> 4.09 us
  transfers between devices with their start and end apart: 10 -> 10, of which waited for: 3 -> 3; matrix products, arithmetic and copies ran while one was open for 0% -> 0% of each run, Pallas kernels for 7% -> 6%
where the time goes in v2:
time: 91.5 us; the launch traced here: 90.9 us
  starting transfers between devices  50.7 us (55%)
  Pallas kernels  20.4 us (22%)
  waiting for transfers between devices  14.8 us (16%)
  local copies, waits for them, and re-layouts  4.09 us (4%)
    ppermute x8, starting transfers between devices, pair_up(): return lax.ppermute(x, axis, pairs)  33.7 us
    pallas_call x8, Pallas kernels, run(): pl.pallas_call(kernel, out_shape=outs, in_specs=[from_hbm] * hbm + [in_vm...  20.4 us
    all_to_all x1, starting transfers between devices, local(): params = lax.all_to_all(params, 'gy', 0, 0, tiled=True)  9.61 us
    all_to_all x1, waiting for transfers between devices, local(): back = lax.all_to_all(back, 'gy', 0, 0, tiled=True)  7.98 us
    all_to_all x1, starting transfers between devices, local(): back = lax.all_to_all(back, 'gy', 0, 0, tiled=True)  7.32 us
    all_to_all x1, waiting for transfers between devices, local(): params = lax.all_to_all(params, 'gy', 0, 0, tiled=True)  5.84 us
    unnamed x24, local copies, waits for them, and re-layouts  4.09 us
  transfers between devices with their start and end apart: 10, of which 3 were waited for; matrix products, arithmetic and copies ran while one was open for 0% of the time, Pallas kernels for 6%

profile of v2, /device:TPU:1, one launch (start us, length us, event | category | flops | bytes accessed | tf_op | source)
XLA Modules:
  0.0 90.9 jit_solution(16491596744020349663)
XLA Ops:
  0.6 1.9 %shard_map.176 = (f32[64,8]{1,0:T(8,128)}, f32[3,56,56]{2,1,0:T(8,128)S(1)}, f32[9,56,128]{2,1,0:T(8,128)S(1)}, f32[9,9,3,128]{3,2,1,0:T(4,128)S(1)}, f32[21,4,5...) custom-call(f32[1,128]{1,0:T(1,128)} %bitcast.35, ...), custom_call_target="tpu_custom_call" | custom-call | tf_op jit(solution)/shard_map/pallas_call | solution.py:466
  2.5 0.0 copy-start.8
  2.5 0.0 copy-start.10
  2.5 0.5 copy-done.8
  3.0 0.0 copy-done.10
  3.0 0.0 copy-start
  3.0 0.0 copy-start.1
  3.0 5.0 %shard_map.177 = (f32[9,56,128]{2,1,0:T(8,128)S(1)}, f32[9,56,128]{2,1,0:T(8,128)S(1)}, f32[96,1152]{1,0:T(8,128)S(1)}, bf16[224,512]{1,0:T(8,128)(2,1)S(1)}, bf...) custom-call(f32[3,56,56]{2,1,0:T(8,128)S(1)} %get-tuple-element.47.s, ...), custom_call_target="tpu_custom_call" | custom-call | tf_op jit(solution)/shard_map/pallas_call | solution.py:466
  8.0 0.0 copy-start.5
  8.0 0.6 copy-done.5
  8.7 4.8 %collective-permute-start = (f32[56,128]{1,0:T(8,128)}, f32[56,128]{1,0:T(8,128)}, u32[]{:S(2)}, u32[]{:S(2)}) collective-permute-start(f32[56,128]{1,0:T(8,128)} %get-tuple-element.60), channel_id=1, source_target_pairs={{0,64},{64,0},{128,192},{192,128},{256,320},{320,256},{384,448},{4... | collective-permute-start | bytes 86024 | tf_op jit(solution)/shard_map/ppermute | solution.py:491
  13.5 12.5 %collective-permute-start.1 = (f32[56,128]{1,0:T(8,128)}, f32[56,128]{1,0:T(8,128)}, u32[]{:S(2)}, u32[]{:S(2)}) collective-permute-start(f32[56,128]{1,0:T(8,128)} %get-tuple-element.61), channel_id=1, source_target_pairs={{0,704},{64,128},{128,64},{192,256},{256,192},{320,384},{384,320},... | collective-permute-start | bytes 86024 | tf_op jit(solution)/shard_map/ppermute | solution.py:491
  26.0 3.1 %collective-permute-start.2 = (f32[56,128]{1,0:T(8,128)}, f32[56,128]{1,0:T(8,128)}, u32[]{:S(2)}, u32[]{:S(2)}) collective-permute-start(f32[56,128]{1,0:T(8,128)} %get-tuple-element.62), channel_id=1, source_target_pairs={{0,1},{1,0},{2,3},{3,2},{4,5},{5,4},{6,7},{7,6},{8,9},{9,8},{10,11... | collective-permute-start | bytes 86024 | tf_op jit(solution)/shard_map/ppermute | solution.py:491
  29.1 3.1 %collective-permute-start.3 = (f32[56,128]{1,0:T(8,128)}, f32[56,128]{1,0:T(8,128)}, u32[]{:S(2)}, u32[]{:S(2)}) collective-permute-start(f32[56,128]{1,0:T(8,128)} %get-tuple-element.63), channel_id=1, source_target_pairs={{0,63},{1,2},{2,1},{3,4},{4,3},{5,6},{6,5},{7,8},{8,7},{9,10},{10,... | collective-permute-start | bytes 86024 | tf_op jit(solution)/shard_map/ppermute | solution.py:491
  32.2 9.6 %all-to-all-start = ((f32[64,1,8]{2,1,0:T(1,128)}), f32[64,1,8]{2,1,0:T(1,128)S(1)}, u32[]{:S(2)}, u32[]{:S(2)}) async-start(f32[64,1,8]{2,1,0:T(1,128)} %bitcast.13), calls=%async_computation | async-start | bytes 65536 | tf_op jit(solution)/shard_map/all_to_all | solution.py:545
  41.9 0.0 copy-done
  41.9 0.0 copy-done.1
  41.9 0.0 copy-start.7
  41.9 0.8 copy-done.7
  42.7 0.0 copy-start.2
  42.7 2.0 %shard_map.178 = (f32[9,56,128]{2,1,0:T(8,128)S(1)}, f32[96,1152]{1,0:T(8,128)S(1)}, f32[224,512]{1,0:T(8,128)S(1)}, bf16[168,256]{1,0:T(8,128)(2,1)S(1)}, bf16[2,56,128]{2,1,0:T(8,128)(2,1)S(1)}) custom-call(f32[9,56,128]{2,1,0:T(8,128)S(1)} %get-tuple-element.52.integral_ref, f32[9,9,3,128]{3,2,1,0:T(4,128)S(1)} %bitcast.22, ...), custom_call_target="tpu_custom_call" | custom-call | tf_op jit(solution)/shard_map/pallas_call | solution.py:466
  44.7 0.0 copy-start.3
  44.7 0.6 copy-done.3
  45.3 5.8 %all-to-all-done = f32[64,1,8]{2,1,0:T(1,128)S(1)} async-done(((f32[64,1,8]{2,1,0:T(1,128)}), f32[64,1,8]{2,1,0:T(1,128)S(1)}, u32[]{:S(2)}, u32[]{:S(2)}) %all-to-all-start) | async-done | bytes 2080 | tf_op jit(solution)/shard_map/all_to_all | solution.py:545
  51.2 0.0 collective-permute-done.m0
  51.2 0.0 collective-permute-done.1.m1
  51.2 0.0 collective-permute-done.2.m2
  51.2 0.0 collective-permute-done.3.m3
  51.2 0.0 copy-start.9
  51.2 0.0 copy-start.11
  51.2 0.0 copy-done.2
  51.2 0.6 copy-done.9
  51.8 0.1 copy-done.11
  51.9 0.0 copy-start.6
  51.9 0.9 copy-done.6
  52.7 0.0 copy-start.4
  52.7 6.3 %shard_map.179 = (f32[9,56,128]{2,1,0:T(8,128)S(1)}, f32[9,56,128]{2,1,0:T(8,128)S(1)}, f32[96,1152]{1,0:T(8,128)S(1)}, bf16[224,512]{1,0:T(8,128)(2,1)S(1)}, bf...) custom-call(f32[9,56,128]{2,1,0:T(8,128)S(1)} %get-tuple-element.46., ...), custom_call_target="tpu_custom_call" | custom-call | tf_op jit(solution)/shard_map/pallas_call | solution.py:466
  59.1 1.9 %collective-permute-start.4 = (f32[56,128]{1,0:T(8,128)S(1)}, f32[56,128]{1,0:T(8,128)S(1)}, u32[]{:S(2)}, u32[]{:S(2)}) collective-permute-start(f32[56,128]{1,0:T(8,128)S(1)} %get-tuple-element.82), channel_id=1, source_target_pairs={{0,64},{64,0},{128,192},{192,128},{256,320},{320,256},{384,448},{4... | collective-permute-start | bytes 86024 | tf_op jit(solution)/shard_map/ppermute | solution.py:491
  61.0 2.8 %collective-permute-start.5 = (f32[56,128]{1,0:T(8,128)S(1)}, f32[56,128]{1,0:T(8,128)S(1)}, u32[]{:S(2)}, u32[]{:S(2)}) collective-permute-start(f32[56,128]{1,0:T(8,128)S(1)} %get-tuple-element.83), channel_id=1, source_target_pairs={{0,704},{64,128},{128,64},{192,256},{256,192},{320,384},{384,320},... | collective-permute-start | bytes 86024 | tf_op jit(solution)/shard_map/ppermute | solution.py:491
  63.8 3.1 %collective-permute-start.6 = (f32[56,128]{1,0:T(8,128)S(1)}, f32[56,128]{1,0:T(8,128)S(1)}, u32[]{:S(2)}, u32[]{:S(2)}) collective-permute-start(f32[56,128]{1,0:T(8,128)S(1)} %get-tuple-element.84), channel_id=1, source_target_pairs={{0,1},{1,0},{2,3},{3,2},{4,5},{5,4},{6,7},{7,6},{8,9},{9,8},{10,11... | collective-permute-start | bytes 86024 | tf_op jit(solution)/shard_map/ppermute | solution.py:491
  67.0 2.3 %collective-permute-start.7 = (f32[56,128]{1,0:T(8,128)S(1)}, f32[56,128]{1,0:T(8,128)S(1)}, u32[]{:S(2)}, u32[]{:S(2)}) collective-permute-start(f32[56,128]{1,0:T(8,128)S(1)} %get-tuple-element.85), channel_id=1, source_target_pairs={{0,63},{1,2},{2,1},{3,4},{4,3},{5,6},{6,5},{7,8},{8,7},{9,10},{10,... | collective-permute-start | bytes 86024 | tf_op jit(solution)/shard_map/ppermute | solution.py:491
  69.3 0.0 copy-done.4
  69.3 1.8 %shard_map.180 = (f32[9,56,128]{2,1,0:T(8,128)S(1)}, f32[96,1152]{1,0:T(8,128)S(1)}, f32[224,512]{1,0:T(8,128)S(1)}) custom-call(f32[9,56,128]{2,1,0:T(8,128)S(1)} %get-tuple-element.74.integral_ref, f32[9,9,3,128]{3,2,1,0:T(4,128)S(1)} %bitcast.24, f32[9,9,4,128]{3,2,1,0:T(4,128)S(1)} %bitcast.26, f32[96,1152]{1,0:T(8,128)S(1)} %get-tuple-element.75.own_ref, ...), custom_call_target="tpu_custom_call" | custom-call | tf_op jit(solution)/shard_map/pallas_call | solution.py:466
  71.1 0.0 collective-permute-done.4.m0
  71.2 0.0 collective-permute-done.5.m1
  71.2 0.0 collective-permute-done.6.m2
  71.2 1.0 %collective-permute-done.7.m3 = f32[56,128]{1,0:T(8,128)S(1)} collective-permute-done((f32[56,128]{1,0:T(8,128)S(1)}, f32[56,128]{1,0:T(8,128)S(1)}, u32[]{:S(2)}, u32[]{:S(2)}) %collective-permute-start.7) | collective-permute-done | bytes 28704 | tf_op jit(solution)/shard_map/ppermute | solution.py:491
  72.2 1.4 %shard_map.181 = (f32[224,512]{1,0:T(8,128)S(1)}, f32[48,512]{1,0:T(8,128)S(1)}, f32[64,8]{1,0:T(8,128)}) custom-call(f32[224,512]{1,0:T(8,128)S(1)} %get-tuple-element.81.near_ref, f32[96,1152]{1,0:T(8,128)S(1)} %get-tuple-element.75.own_ref, f32[56,128]{1,0:T(8,128)S(1)} %collective-permute-done.4.m0, f32[56,128]{1,0:T(8,128)S(1)} %collective-permute-done.5.m1, ...), custom_call_target="tpu_custom_call" | custom-call | tf_op jit(solution)/shard_map/pallas_call | solution.py:466
  73.5 7.3 %all-to-all-start.1 = ((f32[64,1,8]{2,1,0:T(1,128)}), f32[64,1,8]{2,1,0:T(1,128)S(1)}, u32[]{:S(2)}, u32[]{:S(2)}) async-start(f32[64,1,8]{2,1,0:T(1,128)} %bitcast.16), calls=%async_computation.1 | async-start | bytes 65536 | tf_op jit(solution)/shard_map/all_to_all | solution.py:578
  80.9 1.5 %shard_map.182 = f32[9,56,128]{2,1,0:T(8,128)} custom-call(f32[9,56,128]{2,1,0:T(8,128)S(1)} %get-tuple-element.73.base_ref, f32[9,56,128]{2,1,0:T(8,128)S(1)} %get-tuple-element.79.vol_ref, f32[96,1152]{1,0:T(8,128)S(1)} %get-tuple-element.80.part_ref, f32[224,512]{1,0:T(8,128)S(1)} %get-tuple-element.87.nbr_ref, ...), custom_call_target="tpu_custom_call" | custom-call | tf_op jit(solution)/shard_map/pallas_call | solution.py:466
  82.3 8.0 %all-to-all-done.1 = f32[64,1,8]{2,1,0:T(1,128)S(1)} async-done(((f32[64,1,8]{2,1,0:T(1,128)}), f32[64,1,8]{2,1,0:T(1,128)S(1)}, u32[]{:S(2)}, u32[]{:S(2)}) %all-to-all-start.1) | async-done | bytes 2080 | tf_op jit(solution)/shard_map/all_to_all | solution.py:578
  90.3 0.6 shard_map.183
Async XLA Ops:
  2.5 0.5 copy-start.8
  2.5 0.5 copy-start.10
  3.0 38.8 %copy-start = (f32[3,9,9,128]{3,0,2,1:T(4,128)S(1)}, f32[3,9,9,128]{3,0,2,1:T(4,128)}, u32[]{:S(2)}) copy-start(f32[3,9,9,128]{3,0,2,1:T(4,128)} %param.18) | copy-start | bytes 373252
  3.0 38.8 %copy-start.1 = (f32[4,9,9,128]{3,0,2,1:T(4,128)S(1)}, f32[4,9,9,128]{3,0,2,1:T(4,128)}, u32[]{:S(2)}) copy-start(f32[4,9,9,128]{3,0,2,1:T(4,128)} %param.19) | copy-start | bytes 497668
  8.0 0.6 copy-start.5
  8.7 42.5 %collective-permute-start = (f32[56,128]{1,0:T(8,128)}, f32[56,128]{1,0:T(8,128)}, u32[]{:S(2)}, u32[]{:S(2)}) collective-permute-start(f32[56,128]{1,0:T(8,128)} %get-tuple-element.60), channel_id=1, source_target_pairs={{0,64},{64,0},{128,192},{192,128},{256,320},{320,256},{384,448},{4... | collective-permute-start | bytes 86024 | tf_op jit(solution)/shard_map/ppermute | solution.py:491
  13.5 37.7 %collective-permute-start.1 = (f32[56,128]{1,0:T(8,128)}, f32[56,128]{1,0:T(8,128)}, u32[]{:S(2)}, u32[]{:S(2)}) collective-permute-start(f32[56,128]{1,0:T(8,128)} %get-tuple-element.61), channel_id=1, source_target_pairs={{0,704},{64,128},{128,64},{192,256},{256,192},{320,384},{384,320},... | collective-permute-start | bytes 86024 | tf_op jit(solution)/shard_map/ppermute | solution.py:491
  26.0 25.2 %collective-permute-start.2 = (f32[56,128]{1,0:T(8,128)}, f32[56,128]{1,0:T(8,128)}, u32[]{:S(2)}, u32[]{:S(2)}) collective-permute-start(f32[56,128]{1,0:T(8,128)} %get-tuple-element.62), channel_id=1, source_target_pairs={{0,1},{1,0},{2,3},{3,2},{4,5},{5,4},{6,7},{7,6},{8,9},{9,8},{10,11... | collective-permute-start | bytes 86024 | tf_op jit(solution)/shard_map/ppermute | solution.py:491
  29.1 22.0 %collective-permute-start.3 = (f32[56,128]{1,0:T(8,128)}, f32[56,128]{1,0:T(8,128)}, u32[]{:S(2)}, u32[]{:S(2)}) collective-permute-start(f32[56,128]{1,0:T(8,128)} %get-tuple-element.63), channel_id=1, source_target_pairs={{0,63},{1,2},{2,1},{3,4},{4,3},{5,6},{6,5},{7,8},{8,7},{9,10},{10,... | collective-permute-start | bytes 86024 | tf_op jit(solution)/shard_map/ppermute | solution.py:491
  32.2 18.9 %all-to-all-start = ((f32[64,1,8]{2,1,0:T(1,128)}), f32[64,1,8]{2,1,0:T(1,128)S(1)}, u32[]{:S(2)}, u32[]{:S(2)}) async-start(f32[64,1,8]{2,1,0:T(1,128)} %bitcast.13), calls=%async_computation | async-start | bytes 65536 | tf_op jit(solution)/shard_map/all_to_all | solution.py:545
  41.9 0.8 copy-start.7
  42.7 8.6 %copy-start.2 = (f32[4,9,9,128]{3,0,2,1:T(4,128)S(1)}, f32[4,9,9,128]{3,0,2,1:T(4,128)}, u32[]{:S(2)}) copy-start(f32[4,9,9,128]{3,0,2,1:T(4,128)} %param.20) | copy-start | bytes 497668
  44.7 0.6 copy-start.3
  51.2 0.6 copy-start.9
  51.2 0.7 copy-start.11
  51.9 0.9 copy-start.6
  52.7 16.6 %copy-start.4 = (bf16[168,256]{1,0:T(8,128)(2,1)S(1)}, bf16[168,256]{1,0:T(8,128)(2,1)}, u32[]{:S(2)}) copy-start(bf16[168,256]{1,0:T(8,128)(2,1)} %copy-done.3) | copy-start | bytes 258052
  59.1 12.1 %collective-permute-start.4 = (f32[56,128]{1,0:T(8,128)S(1)}, f32[56,128]{1,0:T(8,128)S(1)}, u32[]{:S(2)}, u32[]{:S(2)}) collective-permute-start(f32[56,128]{1,0:T(8,128)S(1)} %get-tuple-element.82), channel_id=1, source_target_pairs={{0,64},{64,0},{128,192},{192,128},{256,320},{320,256},{384,448},{4... | collective-permute-start | bytes 86024 | tf_op jit(solution)/shard_map/ppermute | solution.py:491
  61.0 10.2 %collective-permute-start.5 = (f32[56,128]{1,0:T(8,128)S(1)}, f32[56,128]{1,0:T(8,128)S(1)}, u32[]{:S(2)}, u32[]{:S(2)}) collective-permute-start(f32[56,128]{1,0:T(8,128)S(1)} %get-tuple-element.83), channel_id=1, source_target_pairs={{0,704},{64,128},{128,64},{192,256},{256,192},{320,384},{384,320},... | collective-permute-start | bytes 86024 | tf_op jit(solution)/shard_map/ppermute | solution.py:491
  63.8 7.3 %collective-permute-start.6 = (f32[56,128]{1,0:T(8,128)S(1)}, f32[56,128]{1,0:T(8,128)S(1)}, u32[]{:S(2)}, u32[]{:S(2)}) collective-permute-start(f32[56,128]{1,0:T(8,128)S(1)} %get-tuple-element.84), channel_id=1, source_target_pairs={{0,1},{1,0},{2,3},{3,2},{4,5},{5,4},{6,7},{7,6},{8,9},{9,8},{10,11... | collective-permute-start | bytes 86024 | tf_op jit(solution)/shard_map/ppermute | solution.py:491
  67.0 5.2 %collective-permute-start.7 = (f32[56,128]{1,0:T(8,128)S(1)}, f32[56,128]{1,0:T(8,128)S(1)}, u32[]{:S(2)}, u32[]{:S(2)}) collective-permute-start(f32[56,128]{1,0:T(8,128)S(1)} %get-tuple-element.85), channel_id=1, source_target_pairs={{0,63},{1,2},{2,1},{3,4},{4,3},{5,6},{6,5},{7,8},{8,7},{9,10},{10,... | collective-permute-start | bytes 86024 | tf_op jit(solution)/shard_map/ppermute | solution.py:491
  73.5 16.8 %all-to-all-start.1 = ((f32[64,1,8]{2,1,0:T(1,128)}), f32[64,1,8]{2,1,0:T(1,128)S(1)}, u32[]{:S(2)}, u32[]{:S(2)}) async-start(f32[64,1,8]{2,1,0:T(1,128)} %bitcast.16), calls=%async_computation.1 | async-start | bytes 65536 | tf_op jit(solution)/shard_map/all_to_all | solution.py:578

commit v3 on v2

--- a/solution.py
+++ b/solution.py
@@ -336,12 +336,14 @@
     make_messages(send_ref, high_ref, low_ref, (m0, m1, m2, m3))
 
 
-def near_work(integral_ref, star_ref, own_mats_ref, own_ref, high_ref, low_ref, source_ref, left,
-              vol_ref, flux_ref, near_ref, tall_ref):
+def volume_work(integral_ref, star_ref, left, vol_ref, tall_ref):
     product_of(left, lambda w: integral_ref[w], tall_ref)
     for pair in PAIRS:
         for v, total in zip(pair, star_mix(star_ref, tall_ref, pair)):
             vol_ref[v] = total
+
+
+def near_work(own_mats_ref, own_ref, high_ref, low_ref, source_ref, flux_ref, near_ref):
     mix_faces(own_mats_ref, lambda f, w: own_ref[PTS * f : PTS * (f + 1), lanes(w)], None, flux_ref)
     for f in range(FACES):
         pick = one_hot(iota((FACES * E, E), 0) == source_ref[f : f + 1, :])
@@ -358,25 +360,18 @@
     high, low = halves(jnp.transpose(square_ref[...])[0:MODES])
     al_ref[0] = high
     al_ref[1] = low
-    near_work(integral_ref, star_ref, own_mats_ref, own_ref, high_ref, low_ref, source_ref, av_ref[...],
-              vol_ref, flux_ref, near_ref, tall_ref)
-
-
-def near_second_kernel(
-    integral_ref, star_ref, own_mats_ref, own_ref, high_ref, low_ref, source_ref, av_ref,
-    vol_ref, flux_ref, near_ref,
-    tall_ref,
-):
-    near_work(integral_ref, star_ref, own_mats_ref, own_ref, high_ref, low_ref, source_ref, av_ref[...],
-              vol_ref, flux_ref, near_ref, tall_ref)
+    volume_work(integral_ref, star_ref, av_ref[...], vol_ref, tall_ref)
+    near_work(own_mats_ref, own_ref, high_ref, low_ref, source_ref, flux_ref, near_ref)
 
 
 def middle_kernel(
-    wave_ref, late_ref, vol_ref, part_ref, near_ref, own_ref, m0, m1, m2, m3, nbr_mats_ref, source_ref,
+    wave_hbm, late_ref, vol_ref, part_ref, near_ref, own_ref, m0, m1, m2, m3, nbr_mats_ref, source_ref,
     faces_ref, owner_ref, params_ref, star_ref, ap_ref, at_ref, al_ref, send_ref, cluster_ref, yield_ref, mask_ref,
     integral_ref, base_ref, own2_ref, high_ref, low_ref, n0, n1, n2, n3, par_ref,
-    nbr_ref, state_ref, flux_ref, lifted_ref, mid_ref, tall_a, tall_b, table_ref,
+    nbr_ref, state_ref, flux_ref, lifted_ref, mid_ref, tall_a, tall_b, table_ref, wave_ref, sem,
 ):
+    copy = pltpu.make_async_copy(wave_hbm, wave_ref, sem)
+    copy.start()
     finish_gather(source_ref, (m0, m1, m2, m3), near_ref, nbr_ref)
     faces_row = faces_ref[...]
     state = face_state(own_ref, nbr_ref, faces_row, state_ref)
@@ -392,6 +387,7 @@
     )
     add_change(flux_ref, delta)
     lift(al_ref, flux_ref, lifted_ref)
+    copy.wait()
     coarse = cluster_ref[...] == 1
     for v in range(VARS):
         increment = vol_ref[v] - lifted_ref[:, lanes(v)]
@@ -433,13 +429,17 @@
 
 
 def last_kernel(
-    base_ref, vol_ref, part_ref, nbr_ref, delta_ref, nbr_mats_ref, al_ref, yield_ref, mask_ref,
+    star_hbm, base_ref, integral_ref, av_ref, part_ref, nbr_ref, delta_ref, nbr_mats_ref, al_ref, yield_ref, mask_ref,
     out_ref,
-    flux_ref, lifted_ref,
+    vol_ref, tall_ref, flux_ref, lifted_ref, star_ref, sem,
 ):
+    copy = pltpu.make_async_copy(star_hbm, star_ref, sem)
+    copy.start()
     mix_faces(
         nbr_mats_ref, lambda f, w: nbr_ref[PTS * w : PTS * (w + 1), lanes(f)], part_ref, flux_ref
     )
+    copy.wait()
+    volume_work(integral_ref, star_ref, av_ref[...], vol_ref, tall_ref)
     add_change(flux_ref, delta_ref[...])
     lift(al_ref, flux_ref, lifted_ref)
     for v in range(VARS):
@@ -540,7 +540,7 @@
         [(x.shape, x.dtype) for x in slots],
         hbm=3 + len(firsts),
     )(*(in_hbm(x) for x in (*slots, *firsts)))
-    stiffness, wavefield, star_first, proj = brought[0:4]
+    stiffness, wave_first, star_first, proj = brought[0:4]
     send_faces, face_source, fault_faces, owner, cluster, yield_stress, plastic_mask = brought[4:]
     params = lax.all_to_all(params, "gy", 0, 0, tiled=True)
 
@@ -551,7 +551,7 @@
         [shape(FIELD), shape(FIELD), shape(TRACE), shape(TABLE, BF16), shape(TABLE, BF16), *messages,
          shape(LEFT, BF16), shape((FACES * PTS, 256), BF16)],
         work + [((3 * MODES, E), F32), ((E, E), F32), (TABLE, F32)],
-    )(stiffness, wavefield, star_first, proj, send_faces)
+    )(stiffness, wave_first, star_first, proj, send_faces)
     got = exchange((m0, m1, m2, m3))
     vol, part, near, av, al = call(
         near_first_kernel,
@@ -563,22 +563,24 @@
         [shape(FIELD), shape(FIELD), shape(TRACE), shape(TABLE, BF16), shape(TABLE, BF16), *messages,
          shape((8, faults))],
         [(TABLE, F32), ((3 * PTS + 8, FACES * E), F32), (TRACE, F32), ((MODES, WIDE), F32), (FIELD, F32)]
-        + work + [(TABLE, F32)],
-    )(wavefield, late, vol, part, near, own, *got, nbr_mats, face_source, fault_faces, owner, params, star,
+        + work + [(TABLE, F32), (FIELD, F32)],
+        hbm=1,
+    )(in_hbm(wavefield), late, vol, part, near, own, *got, nbr_mats, face_source, fault_faces, owner, params, star,
       ap, at, al, send_faces, cluster, yield_stress, plastic_mask)
     got = exchange((m0, m1, m2, m3))
-    vol, part, near = call(
-        near_second_kernel, [shape(FIELD), shape(TRACE), shape(TABLE)], work[1:]
-    )(integral, star, own_mats, own, high, low, face_source, av)
+    part, near = call(near_work, [shape(TRACE), shape(TABLE)])(own_mats, own, high, low, face_source)
     nbr, delta, back = call(
         fault_kernel,
         [shape(TABLE), shape((2 * PTS, FACES * E)), shape((gy_size, 8))],
         [((3 * PTS + 8, FACES * E), F32)],
     )(near, own, *got, face_source, fault_faces, owner, params, par)
     back = lax.all_to_all(back, "gy", 0, 0, tiled=True)
-    out = call(last_kernel, shape(FIELD), [(TRACE, F32), ((MODES, WIDE), F32)])(
-        base, vol, part, nbr, delta, nbr_mats, al, yield_stress, plastic_mask
-    )
+    out = call(
+        last_kernel,
+        shape(FIELD),
+        [(FIELD, F32), (TALL, F32), (TRACE, F32), ((MODES, WIDE), F32), (star.shape, F32)],
+        hbm=1,
+    )(in_hbm(star), base, integral, av, part, nbr, delta, nbr_mats, al, yield_stress, plastic_mask)
     slip_out = call(slip_kernel, shape((1, slot_count)))(back)
     return (out, slip_out.reshape(slot_count))
 

time: 91.5 us -> 94 us (1.027)
  local copies, waits for them, and re-layouts: 4.09 us -> 5.23 us
  waiting for transfers between devices: 14.8 us -> 15.9 us
    all_to_all x1, waiting for transfers between devices: 5.84 us -> 7.17 us  [local(): params = lax.all_to_all(params, 'gy', 0, 0, tiled=True)]
    unnamed x24 -> x36, local copies, waits for them, and re-layouts: 4.09 us -> 5.23 us
    all_to_all x1, waiting for transfers between devices: 7.98 us -> 6.92 us  [local(): back = lax.all_to_all(back, 'gy', 0, 0, tiled=True)]
where the time goes in v3:
time: 94 us; the launch traced here: 93.3 us
  starting transfers between devices  50.7 us (54%)
  Pallas kernels  20.7 us (22%)
  waiting for transfers between devices  15.9 us (17%)
  local copies, waits for them, and re-layouts  5.23 us (6%)
    ppermute x8, starting transfers between devices, pair_up(): return lax.ppermute(x, axis, pairs)  33.8 us
    pallas_call x8, Pallas kernels, run(): pl.pallas_call(kernel, out_shape=outs, in_specs=[from_hbm] * hbm + [in_vm...  20.7 us
    all_to_all x1, starting transfers between devices, local(): params = lax.all_to_all(params, 'gy', 0, 0, tiled=True)  9.61 us
    all_to_all x1, starting transfers between devices, local(): back = lax.all_to_all(back, 'gy', 0, 0, tiled=True)  7.29 us
    all_to_all x1, waiting for transfers between devices, local(): params = lax.all_to_all(params, 'gy', 0, 0, tiled=True)  7.17 us
    all_to_all x1, waiting for transfers between devices, local(): back = lax.all_to_all(back, 'gy', 0, 0, tiled=True)  6.92 us
    unnamed x36, local copies, waits for them, and re-layouts  5.23 us
  transfers between devices with their start and end apart: 10, of which 3 were waited for; matrix products, arithmetic and copies ran while one was open for 0% of the time, Pallas kernels for 6%

profile of v3, /device:TPU:1, one launch (start us, length us, event | category | flops | bytes accessed | tf_op | source)
XLA Modules:
  0.0 93.3 jit_solution(9287319780770595025)
XLA Ops:
  0.6 1.9 %shard_map.176 = (f32[64,8]{1,0:T(8,128)}, f32[3,56,56]{2,1,0:T(8,128)S(1)}, f32[9,56,128]{2,1,0:T(8,128)S(1)}, f32[9,9,3,128]{3,2,1,0:T(4,128)S(1)}, f32[21,4,5...) custom-call(f32[1,128]{1,0:T(1,128)} %bitcast.35, ...), custom_call_target="tpu_custom_call" | custom-call | tf_op jit(solution)/shard_map/pallas_call | solution.py:466
  2.5 0.0 copy-start.8
  2.5 0.5 copy-done.8
  3.0 0.0 copy-start.10
  3.0 0.5 copy-done.10
  3.5 0.0 copy-start.12
  3.5 0.5 copy-done.12
  4.1 0.0 copy-start.14
  4.1 0.5 copy-done.14
  4.6 0.0 copy-start.16
  4.6 0.6 copy-done.16
  5.2 0.0 copy-start.6
  5.2 0.6 copy-done.6
  5.7 0.0 copy-start
  5.7 0.0 copy-start.1
  5.8 5.0 %shard_map.177 = (f32[9,56,128]{2,1,0:T(8,128)S(1)}, f32[9,56,128]{2,1,0:T(8,128)S(1)}, f32[96,1152]{1,0:T(8,128)S(1)}, bf16[224,512]{1,0:T(8,128)(2,1)S(1)}, bf...) custom-call(f32[3,56,56]{2,1,0:T(8,128)S(1)} %get-tuple-element.45.s, ...), custom_call_target="tpu_custom_call" | custom-call | tf_op jit(solution)/shard_map/pallas_call | solution.py:466
  10.7 4.8 %collective-permute-start = (f32[56,128]{1,0:T(8,128)}, f32[56,128]{1,0:T(8,128)S(1)}, u32[]{:S(2)}, u32[]{:S(2)}) collective-permute-start(f32[56,128]{1,0:T(8,128)} %get-tuple-element.59), channel_id=1, source_target_pairs={{0,64},{64,0},{128,192},{192,128},{256,320},{320,256},{384,448},{4... | collective-permute-start | bytes 86024 | tf_op jit(solution)/shard_map/ppermute | solution.py:491
  15.5 0.0 copy-start.3
  15.6 12.5 %collective-permute-start.1 = (f32[56,128]{1,0:T(8,128)}, f32[56,128]{1,0:T(8,128)S(1)}, u32[]{:S(2)}, u32[]{:S(2)}) collective-permute-start(f32[56,128]{1,0:T(8,128)} %get-tuple-element.60), channel_id=1, source_target_pairs={{0,704},{64,128},{128,64},{192,256},{256,192},{320,384},{384,320},... | collective-permute-start | bytes 86024 | tf_op jit(solution)/shard_map/ppermute | solution.py:491
  28.0 3.2 %collective-permute-start.2 = (f32[56,128]{1,0:T(8,128)}, f32[56,128]{1,0:T(8,128)}, u32[]{:S(2)}, u32[]{:S(2)}) collective-permute-start(f32[56,128]{1,0:T(8,128)} %get-tuple-element.61), channel_id=1, source_target_pairs={{0,1},{1,0},{2,3},{3,2},{4,5},{5,4},{6,7},{7,6},{8,9},{9,8},{10,11... | collective-permute-start | bytes 86024 | tf_op jit(solution)/shard_map/ppermute | solution.py:491
  31.2 3.1 %collective-permute-start.3 = (f32[56,128]{1,0:T(8,128)}, f32[56,128]{1,0:T(8,128)}, u32[]{:S(2)}, u32[]{:S(2)}) collective-permute-start(f32[56,128]{1,0:T(8,128)} %get-tuple-element.62), channel_id=1, source_target_pairs={{0,63},{1,2},{2,1},{3,4},{4,3},{5,6},{6,5},{7,8},{8,7},{9,10},{10,... | collective-permute-start | bytes 86024 | tf_op jit(solution)/shard_map/ppermute | solution.py:491
  34.3 9.6 %all-to-all-start = ((f32[64,1,8]{2,1,0:T(1,128)}), f32[64,1,8]{2,1,0:T(1,128)S(1)}, u32[]{:S(2)}, u32[]{:S(2)}) async-start(f32[64,1,8]{2,1,0:T(1,128)} %bitcast.13), calls=%async_computation | async-start | bytes 65536 | tf_op jit(solution)/shard_map/all_to_all | solution.py:545
  43.9 0.0 copy-done
  43.9 0.0 copy-done.1
  43.9 0.0 copy-done.3
  44.0 0.0 copy-start.2
  44.0 2.0 %shard_map.178 = (f32[9,56,128]{2,1,0:T(8,128)S(1)}, f32[96,1152]{1,0:T(8,128)S(1)}, f32[224,512]{1,0:T(8,128)S(1)}, bf16[168,256]{1,0:T(8,128)(2,1)S(1)}, bf16[2,56,128]{2,1,0:T(8,128)(2,1)S(1)}) custom-call(f32[9,56,128]{2,1,0:T(8,128)S(1)} %get-tuple-element.51.integral_ref, f32[9,9,3,128]{3,2,1,0:T(4,128)S(1)} %bitcast.23, ...), custom_call_target="tpu_custom_call" | custom-call | tf_op jit(solution)/shard_map/pallas_call | solution.py:466
  46.0 7.2 %all-to-all-done = f32[64,1,8]{2,1,0:T(1,128)S(1)} async-done(((f32[64,1,8]{2,1,0:T(1,128)}), f32[64,1,8]{2,1,0:T(1,128)S(1)}, u32[]{:S(2)}, u32[]{:S(2)}) %all-to-all-start) | async-done | bytes 2080 | tf_op jit(solution)/shard_map/all_to_all | solution.py:545
  53.2 0.0 collective-permute-done.m0
  53.2 0.0 collective-permute-done.1.m1
  53.2 0.0 copy-start.4
  53.2 0.6 copy-done.4
  53.8 0.0 collective-permute-done.2.m2
  53.8 0.0 collective-permute-done.3.m3
  53.8 0.0 copy-start.15
  53.8 0.0 copy-start.17
  53.8 0.0 copy-start.7
  53.8 0.0 copy-start.9
  53.8 0.0 copy-start.11
  53.8 0.0 copy-start.13
  53.8 0.0 copy-done.2
  53.9 0.6 copy-done.15
  54.4 0.1 copy-done.17
  54.5 0.0 copy-done.7
  54.5 0.0 copy-done.9
  54.5 0.0 copy-done.11
  54.5 0.0 copy-done.13
  54.5 0.0 copy-start.5
  54.5 0.7 copy-done.5
  55.2 6.3 %shard_map.179 = (f32[9,56,128]{2,1,0:T(8,128)S(1)}, f32[9,56,128]{2,1,0:T(8,128)S(1)}, f32[96,1152]{1,0:T(8,128)S(1)}, bf16[224,512]{1,0:T(8,128)(2,1)S(1)}, bf...) custom-call(f32[9,56,128]{2,1,0:T(8,128)} %wave_hbm.1, ...), custom_call_target="tpu_custom_call" | custom-call | tf_op jit(solution)/shard_map/pallas_call | solution.py:466
  61.5 1.9 %collective-permute-start.4 = (f32[56,128]{1,0:T(8,128)S(1)}, f32[56,128]{1,0:T(8,128)S(1)}, u32[]{:S(2)}, u32[]{:S(2)}) collective-permute-start(f32[56,128]{1,0:T(8,128)S(1)} %get-tuple-element.80), channel_id=1, source_target_pairs={{0,64},{64,0},{128,192},{192,128},{256,320},{320,256},{384,448},{4... | collective-permute-start | bytes 86024 | tf_op jit(solution)/shard_map/ppermute | solution.py:491
  63.5 2.8 %collective-permute-start.5 = (f32[56,128]{1,0:T(8,128)S(1)}, f32[56,128]{1,0:T(8,128)S(1)}, u32[]{:S(2)}, u32[]{:S(2)}) collective-permute-start(f32[56,128]{1,0:T(8,128)S(1)} %get-tuple-element.81), channel_id=1, source_target_pairs={{0,704},{64,128},{128,64},{192,256},{256,192},{320,384},{384,320},... | collective-permute-start | bytes 86024 | tf_op jit(solution)/shard_map/ppermute | solution.py:491
  66.3 3.1 %collective-permute-start.6 = (f32[56,128]{1,0:T(8,128)S(1)}, f32[56,128]{1,0:T(8,128)S(1)}, u32[]{:S(2)}, u32[]{:S(2)}) collective-permute-start(f32[56,128]{1,0:T(8,128)S(1)} %get-tuple-element.82), channel_id=1, source_target_pairs={{0,1},{1,0},{2,3},{3,2},{4,5},{5,4},{6,7},{7,6},{8,9},{9,8},{10,11... | collective-permute-start | bytes 86024 | tf_op jit(solution)/shard_map/ppermute | solution.py:491
  69.4 2.3 %collective-permute-start.7 = (f32[56,128]{1,0:T(8,128)S(1)}, f32[56,128]{1,0:T(8,128)S(1)}, u32[]{:S(2)}, u32[]{:S(2)}) collective-permute-start(f32[56,128]{1,0:T(8,128)S(1)} %get-tuple-element.83), channel_id=1, source_target_pairs={{0,63},{1,2},{2,1},{3,4},{4,3},{5,6},{6,5},{7,8},{8,7},{9,10},{10,... | collective-permute-start | bytes 86024 | tf_op jit(solution)/shard_map/ppermute | solution.py:491
  71.8 1.0 %shard_map.180 = (f32[96,1152]{1,0:T(8,128)S(1)}, f32[224,512]{1,0:T(8,128)S(1)}) custom-call(f32[9,9,4,128]{3,2,1,0:T(4,128)S(1)} %bitcast.26, f32[96,1152]{1,0:T(8,128)S(1)} %get-tuple-element.75.own_ref, bf16[224,512]{1,0:T(8,128)(2,1)S(1)} %get-tuple-element.76.high_ref, bf16[224,512]{1,0:T(8,128)(2,1)S(1)} %get-tuple-element.77.low_ref, ...), custom_call_target="tpu_custom_call" | custom-call | tf_op jit(solution)/shard_map/pallas_call | solution.py:466
  72.8 0.0 collective-permute-done.4.m0
  72.8 0.0 collective-permute-done.5.m1
  72.9 0.0 collective-permute-done.6.m2
  72.9 1.8 %collective-permute-done.7.m3 = f32[56,128]{1,0:T(8,128)S(1)} collective-permute-done((f32[56,128]{1,0:T(8,128)S(1)}, f32[56,128]{1,0:T(8,128)S(1)}, u32[]{:S(2)}, u32[]{:S(2)}) %collective-permute-start.7) | collective-permute-done | bytes 28704 | tf_op jit(solution)/shard_map/ppermute | solution.py:491
  74.6 1.4 %shard_map.181 = (f32[224,512]{1,0:T(8,128)S(1)}, f32[48,512]{1,0:T(8,128)S(1)}, f32[64,8]{1,0:T(8,128)}) custom-call(f32[224,512]{1,0:T(8,128)S(1)} %get-tuple-element.79.near_ref, f32[96,1152]{1,0:T(8,128)S(1)} %get-tuple-element.75.own_ref, f32[56,128]{1,0:T(8,128)S(1)} %collective-permute-done.4.m0, f32[56,128]{1,0:T(8,128)S(1)} %collective-permute-done.5.m1, ...), custom_call_target="tpu_custom_call" | custom-call | tf_op jit(solution)/shard_map/pallas_call | solution.py:466
  76.0 7.3 %all-to-all-start.1 = ((f32[64,1,8]{2,1,0:T(1,128)}), f32[64,1,8]{2,1,0:T(1,128)S(1)}, u32[]{:S(2)}, u32[]{:S(2)}) async-start(f32[64,1,8]{2,1,0:T(1,128)} %bitcast.16), calls=%async_computation.1 | async-start | bytes 65536 | tf_op jit(solution)/shard_map/all_to_all | solution.py:577
  83.3 2.5 %shard_map.182 = f32[9,56,128]{2,1,0:T(8,128)} custom-call(f32[9,9,3,128]{3,2,1,0:T(4,128)} %bitcast.22, f32[9,56,128]{2,1,0:T(8,128)S(1)} %get-tuple-element.72.base_ref, f32[9,56,128]{2,1,0:T(8,128)S(1)} %get-tuple-element.73.integral_ref, bf16[168,256]{1,0:T(8,128)(2,1)S(1)} %get-tuple-element.74.av_ref, f32[96,1152]{1,0:T(8,128)S(1)} %get-tuple-element.78.part_ref, ...), custom_call_target="tpu_custom_call" | custom-call | tf_op jit(solution)/shard_map/pallas_call | solution.py:466
  85.8 6.9 %all-to-all-done.1 = f32[64,1,8]{2,1,0:T(1,128)S(1)} async-done(((f32[64,1,8]{2,1,0:T(1,128)}), f32[64,1,8]{2,1,0:T(1,128)S(1)}, u32[]{:S(2)}, u32[]{:S(2)}) %all-to-all-start.1) | async-done | bytes 2080 | tf_op jit(solution)/shard_map/all_to_all | solution.py:577
  92.7 0.6 shard_map.183
Async XLA Ops:
  2.5 0.5 copy-start.8
  3.0 0.5 copy-start.10
  3.5 0.5 copy-start.12
  4.1 0.5 copy-start.14
  4.6 0.6 copy-start.16
  5.2 0.6 copy-start.6
  5.7 38.2 %copy-start = (f32[3,9,9,128]{3,0,2,1:T(4,128)S(1)}, f32[3,9,9,128]{3,0,2,1:T(4,128)}, u32[]{:S(2)}) copy-start(f32[3,9,9,128]{3,0,2,1:T(4,128)} %param.18) | copy-start | bytes 373252
  5.7 38.2 %copy-start.1 = (f32[4,9,9,128]{3,0,2,1:T(4,128)S(1)}, f32[4,9,9,128]{3,0,2,1:T(4,128)}, u32[]{:S(2)}) copy-start(f32[4,9,9,128]{3,0,2,1:T(4,128)} %param.19) | copy-start | bytes 497668
  10.7 42.4 %collective-permute-start = (f32[56,128]{1,0:T(8,128)}, f32[56,128]{1,0:T(8,128)S(1)}, u32[]{:S(2)}, u32[]{:S(2)}) collective-permute-start(f32[56,128]{1,0:T(8,128)} %get-tuple-element.59), channel_id=1, source_target_pairs={{0,64},{64,0},{128,192},{192,128},{256,320},{320,256},{384,448},{4... | collective-permute-start | bytes 86024 | tf_op jit(solution)/shard_map/ppermute | solution.py:491
  15.5 28.4 %copy-start.3 = (f32[4,56,21]{1,0,2:T(4,128)S(1)}, f32[4,56,21]{1,0,2:T(4,128)}, u32[]{:S(2)}) copy-start(f32[4,56,21]{1,0,2:T(4,128)} %param.23) | copy-start | bytes 56452
  15.6 37.6 %collective-permute-start.1 = (f32[56,128]{1,0:T(8,128)}, f32[56,128]{1,0:T(8,128)S(1)}, u32[]{:S(2)}, u32[]{:S(2)}) collective-permute-start(f32[56,128]{1,0:T(8,128)} %get-tuple-element.60), channel_id=1, source_target_pairs={{0,704},{64,128},{128,64},{192,256},{256,192},{320,384},{384,320},... | collective-permute-start | bytes 86024 | tf_op jit(solution)/shard_map/ppermute | solution.py:491
  28.0 25.7 %collective-permute-start.2 = (f32[56,128]{1,0:T(8,128)}, f32[56,128]{1,0:T(8,128)}, u32[]{:S(2)}, u32[]{:S(2)}) collective-permute-start(f32[56,128]{1,0:T(8,128)} %get-tuple-element.61), channel_id=1, source_target_pairs={{0,1},{1,0},{2,3},{3,2},{4,5},{5,4},{6,7},{7,6},{8,9},{9,8},{10,11... | collective-permute-start | bytes 86024 | tf_op jit(solution)/shard_map/ppermute | solution.py:491
  31.2 22.6 %collective-permute-start.3 = (f32[56,128]{1,0:T(8,128)}, f32[56,128]{1,0:T(8,128)}, u32[]{:S(2)}, u32[]{:S(2)}) collective-permute-start(f32[56,128]{1,0:T(8,128)} %get-tuple-element.62), channel_id=1, source_target_pairs={{0,63},{1,2},{2,1},{3,4},{4,3},{5,6},{6,5},{7,8},{8,7},{9,10},{10,... | collective-permute-start | bytes 86024 | tf_op jit(solution)/shard_map/ppermute | solution.py:491
  34.3 18.9 %all-to-all-start = ((f32[64,1,8]{2,1,0:T(1,128)}), f32[64,1,8]{2,1,0:T(1,128)S(1)}, u32[]{:S(2)}, u32[]{:S(2)}) async-start(f32[64,1,8]{2,1,0:T(1,128)} %bitcast.13), calls=%async_computation | async-start | bytes 65536 | tf_op jit(solution)/shard_map/all_to_all | solution.py:545
  44.0 9.9 %copy-start.2 = (f32[4,9,9,128]{3,0,2,1:T(4,128)S(1)}, f32[4,9,9,128]{3,0,2,1:T(4,128)}, u32[]{:S(2)}) copy-start(f32[4,9,9,128]{3,0,2,1:T(4,128)} %param.20) | copy-start | bytes 497668
  53.2 0.6 copy-start.4
  53.8 0.6 copy-start.15
  53.8 0.7 copy-start.17
  53.8 0.7 copy-start.7
  53.8 0.7 copy-start.9
  53.8 0.7 copy-start.11
  53.8 0.7 copy-start.13
  54.5 0.7 copy-start.5
  61.5 11.3 %collective-permute-start.4 = (f32[56,128]{1,0:T(8,128)S(1)}, f32[56,128]{1,0:T(8,128)S(1)}, u32[]{:S(2)}, u32[]{:S(2)}) collective-permute-start(f32[56,128]{1,0:T(8,128)S(1)} %get-tuple-element.80), channel_id=1, source_target_pairs={{0,64},{64,0},{128,192},{192,128},{256,320},{320,256},{384,448},{4... | collective-permute-start | bytes 86024 | tf_op jit(solution)/shard_map/ppermute | solution.py:491
  63.5 9.4 %collective-permute-start.5 = (f32[56,128]{1,0:T(8,128)S(1)}, f32[56,128]{1,0:T(8,128)S(1)}, u32[]{:S(2)}, u32[]{:S(2)}) collective-permute-start(f32[56,128]{1,0:T(8,128)S(1)} %get-tuple-element.81), channel_id=1, source_target_pairs={{0,704},{64,128},{128,64},{192,256},{256,192},{320,384},{384,320},... | collective-permute-start | bytes 86024 | tf_op jit(solution)/shard_map/ppermute | solution.py:491
  66.3 6.6 %collective-permute-start.6 = (f32[56,128]{1,0:T(8,128)S(1)}, f32[56,128]{1,0:T(8,128)S(1)}, u32[]{:S(2)}, u32[]{:S(2)}) collective-permute-start(f32[56,128]{1,0:T(8,128)S(1)} %get-tuple-element.82), channel_id=1, source_target_pairs={{0,1},{1,0},{2,3},{3,2},{4,5},{5,4},{6,7},{7,6},{8,9},{9,8},{10,11... | collective-permute-start | bytes 86024 | tf_op jit(solution)/shard_map/ppermute | solution.py:491
  69.4 5.2 %collective-permute-start.7 = (f32[56,128]{1,0:T(8,128)S(1)}, f32[56,128]{1,0:T(8,128)S(1)}, u32[]{:S(2)}, u32[]{:S(2)}) collective-permute-start(f32[56,128]{1,0:T(8,128)S(1)} %get-tuple-element.83), channel_id=1, source_target_pairs={{0,63},{1,2},{2,1},{3,4},{4,3},{5,6},{6,5},{7,8},{8,7},{9,10},{10,... | collective-permute-start | bytes 86024 | tf_op jit(solution)/shard_map/ppermute | solution.py:491
  76.0 16.7 %all-to-all-start.1 = ((f32[64,1,8]{2,1,0:T(1,128)}), f32[64,1,8]{2,1,0:T(1,128)S(1)}, u32[]{:S(2)}, u32[]{:S(2)}) async-start(f32[64,1,8]{2,1,0:T(1,128)} %bitcast.16), calls=%async_computation.1 | async-start | bytes 65536 | tf_op jit(solution)/shard_map/all_to_all | solution.py:577
